TPU v7x, 32 devices: a whole 2x2x4 slice. The times are simulated.
32 devices in a mesh: batch: 8 (over z, x), tensor: 4 (over y, core).
Axes of the slice: x: 2, y: 2, z: 4, core: 2. Of those that a mesh axis runs over, the one named last changes fastest.
Arguments:
- token_ids: int32 [8, 1024], P('batch'), may hold values from 0 to 50303
- targets: int32 [8, 1024], P('batch'), may hold values from 0 to 50303
- task_groups: int32 [8], P('batch'), may hold values from 0 to 3, as said below
- embedding: bfloat16 [50304, 1024], P('tensor'), may hold values from -0.3984375 to 0.3984375
- positions: bfloat16 [1024, 1024], replicated, may hold values from -0.59765625 to 0.59765625
- norm_gains: float32 [3, 1024], replicated, may hold values from 0.5 to 1.5
- norm_shifts: float32 [3, 1024], replicated, may hold values from -1.2 to 1.2
- w_qkv: bfloat16 [1024, 3, 1024], P(None, None, 'tensor'), may hold values from -0.1875 to 0.1875
- attention_output_weight: bfloat16 [1024, 1024], P('tensor'), may hold values from -0.375 to 0.375
- expand_weight: bfloat16 [1024, 4096], P(None, 'tensor'), may hold values from -0.1875 to 0.1875
- contract_weight: bfloat16 [4096, 1024], P('tensor'), may hold values from -0.046875 to 0.046875
- model_down_maps: float32 [5, 1024, 4], replicated, may hold values from -0.1875 to 0.1875
- hidden_down_map: float32 [4096, 4], replicated, may hold values from -0.09375 to 0.09375
- model_up_maps: float32 [5, 4, 1024], replicated, may hold values from -0.18 to 0.18
- hidden_up_map: float32 [4, 4096], replicated, may hold values from -0.18 to 0.18
- model_down_first: float32 [5, 1024, 4], replicated, may hold values from -5.722046e-06 to 5.722046e-06
- hidden_down_first: float32 [4096, 4], replicated, may hold values from -5.722046e-06 to 5.722046e-06
- model_up_first: float32 [5, 4, 1024], replicated, may hold values from -5.722046e-06 to 5.722046e-06
- hidden_up_first: float32 [4, 4096], replicated, may hold values from -5.722046e-06 to 5.722046e-06
- model_down_second: float32 [5, 1024, 4], replicated, may hold values from 1.3563368e-14 to 5.4253473e-14
- hidden_down_second: float32 [4096, 4], replicated, may hold values from 1.3563368e-14 to 5.4253473e-14
- model_up_second: float32 [5, 4, 1024], replicated, may hold values from 1.3563368e-14 to 5.4253473e-14
- hidden_up_second: float32 [4, 4096], replicated, may hold values from 1.3563368e-14 to 5.4253473e-14
Outputs:
- loss: float32 [], replicated
- grad_norm: float32 [], replicated
- a_model_new: float32 [5, 1024, 4], replicated
- a_hidden_new: float32 [4096, 4], replicated
- b_model_new: float32 [5, 4, 1024], replicated
- b_hidden_new: float32 [4, 4096], replicated
- a_model_m_new: float32 [5, 1024, 4], replicated
- a_hidden_m_new: float32 [4096, 4], replicated
- b_model_m_new: float32 [5, 4, 1024], replicated
- b_hidden_m_new: float32 [4, 4096], replicated
- a_model_v_new: float32 [5, 1024, 4], replicated
- a_hidden_v_new: float32 [4096, 4], replicated
- b_model_v_new: float32 [5, 4, 1024], replicated
- b_hidden_v_new: float32 [4, 4096], replicated
Inputs may be any that keep to these rules, and one draw needn't show every extreme that they name: `task_groups`: every one of the 4 groups holds at least one sequence.
All inputs are finite; a program needn't handle non-finite values.
Results may differ from a plain program's by a relative error of at most 0.0038.
Values may be sent and summed in bfloat16 or wider, within the bound.
No kernel may reach another device: no remote copies, remote signals or barrier semaphores. Data moves between devices by JAX's collectives and lax.ppermute only.
A program may use at most 192 MiB of HBM per device.

v0:
```python
import functools

import jax
import jax.numpy as jnp
from jax import lax
from jax.experimental import pallas as pl
from jax.experimental.pallas import tpu as pltpu
from jax.sharding import PartitionSpec as P

HEAD_DIM = 64
GROUPS = 4
ADAM_STEP = 5

beta_one = 0.9
beta_two = 0.999
learn_rate = 0.01
decay_rate = 0.01
adam_eps = 1e-08
clip_limit = 0.001
adapter_scale = 8.0
score_scale = HEAD_DIM**-0.5

CHUNKS = 2
VOCAB_BLOCK = 3072

f32 = jnp.float32
bf16 = jnp.bfloat16
NT = (((1,), (1,)), ((), ()))
TN = (((0,), (0,)), ((), ()))
VM = pl.BlockSpec(memory_space=pltpu.VMEM)
SM = pl.BlockSpec(memory_space=pltpu.SMEM)
HBM = pl.BlockSpec(memory_space=pl.ANY)


def mm(left, right):
    return jnp.dot(left, right, preferred_element_type=f32)


def mm_nt(left, right):
    return lax.dot_general(left, right, NT, preferred_element_type=f32)


def mm_tn(left, right):
    return lax.dot_general(left, right, TN, preferred_element_type=f32)


def call(kernel, outs, ins, specs, scratch=(), flops=0, name=None, room=16):
    size = sum(x.size * x.dtype.itemsize for x in ins) + sum(
        x.size * jnp.dtype(x.dtype).itemsize for x in outs
    )
    return pl.pallas_call(
        kernel,
        out_shape=tuple(outs),
        in_specs=specs,
        out_specs=tuple(VM for _ in outs),
        scratch_shapes=list(scratch),
        compiler_params=pltpu.CompilerParams(
            vmem_limit_bytes=min(size + (room << 20), 56 << 20)
        ),
        cost_estimate=pl.CostEstimate(flops=int(flops), bytes_accessed=size, transcendentals=0),
        name=name,
    )(*ins)


def shape(dims, dtype):
    return jax.ShapeDtypeStruct(tuple(dims), dtype)


def split_columns(values, width):
    high = values.astype(bf16)
    column = lax.broadcasted_iota(jnp.int32, values.shape, 1)
    low = (values - high.astype(f32)).astype(bf16)
    return jnp.where((column >= width) & (column < 2 * width), low, high)


def gather_kernel(place_ref, ids_ref, table, *refs):
    outs = refs[:-3]
    buf, sems, counts = refs[-3:]
    side = place_ref[0]
    offset = place_ref[1]
    half, width = outs[0].shape
    vocab = table.shape[0]

    def base(g):
        return (g // 2 * 2 + (side if g % 2 == 0 else 1 - side)) * half

    def find(position):
        local = ids_ref[position] - offset
        return local, (local >= 0) & (local < vocab)

    def fetch(row, slot, g):
        return pltpu.make_async_copy(
            table.at[pl.ds(pl.multiple_of(row, 8), 8)], buf.at[slot], sems.at[g]
        )

    for g in range(len(outs)):

        def start(i, count, g=g):
            local, inside = find(base(g) + i)

            @pl.when(inside)
            def _():
                fetch(jnp.bitwise_and(local, -8), g * half + i, g).start()

            return count + inside.astype(jnp.int32)

        counts[g] = lax.fori_loop(0, half, start, jnp.int32(0), unroll=8)
    sublane = lax.broadcasted_iota(jnp.int32, (8, width), 0)
    for g in range(len(outs)):

        def wait(i, carry, g=g):
            fetch(0, g * half, g).wait()
            return carry

        lax.fori_loop(0, counts[g], wait, 0)

        def extract(i, carry, g=g):
            pieces = []
            for h in range(2):
                rows = jnp.zeros((8, width), f32)
                for j in range(8):
                    t = i * 16 + h * 8 + j
                    local, inside = find(base(g) + t)
                    shift = jnp.bitwise_and(j - local, 7)
                    block = pltpu.roll(buf[g * half + t].astype(f32), shift, 0)
                    rows = jnp.where(sublane == jnp.where(inside, j, -1), block, rows)
                pieces.append(rows)
            outs[g][pl.ds(pl.multiple_of(i * 16, 16), 16), :] = jnp.concatenate(pieces, 0).astype(
                bf16
            )
            return carry

        lax.fori_loop(0, half // 16, extract, 0)


def gather(place, ids, table, half):
    count = ids.shape[0] // half
    width = table.shape[1]
    return pl.pallas_call(
        gather_kernel,
        out_shape=tuple(shape((half, width), bf16) for _ in range(count)),
        in_specs=[SM, SM, HBM],
        out_specs=(VM,) * count,
        scratch_shapes=[
            pltpu.VMEM((count * half, 8, width), bf16),
            pltpu.SemaphoreType.DMA((count,)),
            pltpu.SMEM((count,), jnp.int32),
        ],
        compiler_params=pltpu.CompilerParams(vmem_limit_bytes=28 << 20),
        cost_estimate=pl.CostEstimate(
            flops=1, bytes_accessed=16 * count * half * width, transcendentals=0
        ),
        name="gather",
    )(place, ids, table)


def norm_parts(values):
    centre = jnp.mean(values, -1, keepdims=True)
    centred = values - centre
    spread = jnp.mean(centred * centred, -1, keepdims=True)
    return centred, lax.rsqrt(spread + 1e-05)


def norm_kernel(place, sum_ref, got_ref, x_ref, gain_ref, shift_ref, x_out, h_out):
    values = x_ref[...].astype(f32) + (sum_ref[...].astype(f32) + got_ref[...].astype(f32))
    x_out[...] = values
    centred, inverse = norm_parts(values)
    gain = gain_ref[place : place + 1, :]
    shift = shift_ref[place : place + 1, :]
    h_out[...] = (centred * inverse * gain + shift).astype(bf16)


def norm_forward(place, total, got, x, gains, shifts):
    return call(
        functools.partial(norm_kernel, place),
        [shape(x.shape, f32), shape(x.shape, bf16)],
        [total, got, x, gains, shifts],
        [VM] * 5,
        name=f"norm_forward_{place}",
    )


def norm_derivative(grad, values, gain):
    centred, inverse = norm_parts(values)
    hat = centred * inverse
    scaled = grad * gain
    first = jnp.mean(scaled, -1, keepdims=True)
    second = jnp.mean(scaled * hat, -1, keepdims=True)
    return inverse * (scaled - first - hat * second)


def norm_back_kernel(place, has_rest, sum_ref, got_ref, x_ref, gain_ref, *rest):
    if has_rest:
        rest_ref, dx_out, low_out = rest
    else:
        dx_out, low_out = rest
    grad = sum_ref[...].astype(f32) + got_ref[...].astype(f32)
    dx = norm_derivative(grad, x_ref[...], gain_ref[place : place + 1, :])
    if has_rest:
        dx = dx + rest_ref[...]
    dx_out[...] = dx
    low_out[...] = dx.astype(bf16)


def norm_backward(place, total, got, x, gains, rest=None):
    ins = [total, got, x, gains] + ([] if rest is None else [rest])
    return call(
        functools.partial(norm_back_kernel, place, rest is not None),
        [shape(x.shape, f32), shape(x.shape, bf16)],
        ins,
        [VM] * len(ins),
        name=f"norm_backward_{place}",
    )


def qkv_kernel(side_ref, hm_ref, ho_ref, w_ref, a_ref, b_ref, qkv_out, h_out, u_out):
    side = side_ref[0]
    for h_ref, half in ((hm_ref, side), (ho_ref, 1 - side)):
        h = h_ref[...]
        u = split_columns(mm_nt(h, a_ref[...]), 12)
        h_out[half] = h
        u_out[half] = u
        for j in range(3):
            qkv_out[j, half] = (mm(h, w_ref[j]) + mm(u, b_ref[j])).astype(bf16)


def attention_kernel(
    place, heads, side_ref, wo_ref, a_ref, b_ref, *refs
):
    qkv_refs = refs[: place + 1]
    mine_ref, theirs_ref, o_out, lse_out, u_out, vt, ot = refs[place + 1 :]
    side = side_ref[0]
    _, _, half_rows, width = qkv_refs[0].shape
    rows = 2 * half_rows
    for p in range(place + 1):
        vt[:, p * rows : (p + 1) * rows] = jnp.transpose(
            qkv_refs[p][2].reshape(rows, width).astype(f32)
        ).astype(bf16)
    lane = lax.broadcasted_iota(jnp.int32, (half_rows, width), 1) // HEAD_DIM
    key = lax.broadcasted_iota(jnp.int32, (half_rows, half_rows), 0)
    query = lax.broadcasted_iota(jnp.int32, (half_rows, half_rows), 1)
    causal = key <= query
    for b in range(2):
        keys = [qkv_refs[p][1].reshape(rows, width) for p in range(place)]
        keys += [qkv_refs[place][1, i] for i in range(b + 1)]
        q = (qkv_refs[place][0, b].astype(f32) * score_scale).astype(bf16)
        for head in range(heads):
            q_head = jnp.where(lane == head, q, jnp.zeros_like(q))
            scores = [mm_nt(k, q_head) for k in keys]
            scores[-1] = jnp.where(causal, scores[-1], -1e30)
            peak = functools.reduce(
                jnp.maximum, [jnp.max(s, 0, keepdims=True) for s in scores]
            )
            raised = [jnp.exp(s - peak) for s in scores]
            total = functools.reduce(jnp.add, [jnp.sum(r, 0, keepdims=True) for r in raised])
            inverse = 1.0 / total
            part = None
            start = 0
            for r in raised:
                count = r.shape[0]
                weights = (r * inverse).astype(bf16)
                term = mm(
                    vt[head * HEAD_DIM : (head + 1) * HEAD_DIM, start : start + count], weights
                )
                part = term if part is None else part + term
                start += count
            ot[head * HEAD_DIM : (head + 1) * HEAD_DIM, :] = part
            lse_out[head : head + 1, b * half_rows : (b + 1) * half_rows] = peak + jnp.log(total)
        o = jnp.transpose(ot[...]).astype(bf16)
        u = split_columns(mm_nt(o, a_ref[...]), 4)
        o_out[b] = o
        u_out[b] = u
        part = mm(o, wo_ref[...]) + mm(u, b_ref[...])

        @pl.when(side == b)
        def _():
            mine_ref[...] = part

        @pl.when(side != b)
        def _():
            theirs_ref[...] = part.astype(bf16)


def mlp_kernel(
    hm_ref, ho_ref, we_ref, wc_ref, ae_ref, be_ref, ac_ref, bc_ref,
    mine_ref, theirs_ref, g_out, slope_out, ue_out, uc_out,
):
    for place, h_ref in ((1, ho_ref), (0, hm_ref)):
        h = h_ref[...]
        ue = split_columns(mm_nt(h, ae_ref[...]), 4)
        f = mm(h, we_ref[...]) + mm(ue, be_ref[...])
        square = f * f
        t = jnp.tanh(0.7978845608028654 * (f + 0.044715 * square * f))
        g = (0.5 * f * (1.0 + t)).astype(bf16)
        slope = 0.5 * (1.0 + t) + 0.5 * f * (1.0 - t * t) * (
            0.7978845608028654 + (3.0 * 0.044715 * 0.7978845608028654) * square
        )
        uc = split_columns(mm_nt(g, ac_ref[...]), 4)
        part = mm(g, wc_ref[...]) + mm(uc, bc_ref[...])
        g_out[place] = g
        slope_out[place] = slope
        ue_out[place] = ue
        uc_out[place] = uc
        if place:
            theirs_ref[...] = part.astype(bf16)
        else:
            mine_ref[...] = part


def pack_stats(stats, width):
    high = stats.astype(bf16).astype(f32)
    middle = (stats - high).astype(bf16).astype(f32)
    low = stats - high - middle
    parts = [high, middle, low]
    missing = width - 3 * stats.shape[1]
    if missing:
        parts.append(jnp.zeros((stats.shape[0], missing), f32))
    packed = jnp.concatenate(parts, 1)
    return jnp.concatenate([packed, jnp.zeros_like(packed)], 0).astype(bf16)


def unpack_stats(packed, count):
    wide = packed.astype(f32)[:8]
    return wide[:, :count] + wide[:, count : 2 * count] + wide[:, 2 * count : 3 * count]


def head_kernel(
    block, hm_ref, ho_ref, table, mine_ref, theirs_ref, own_stat,
    buf, tail, sems, peak, total, rows, acc,
):
    tail_rows = tail.shape[0]
    blocks = (table.shape[0] - tail_rows) // block
    half = hm_ref.shape[0]
    count = 2 * half

    def fetch(index, slot):
        start = pl.multiple_of(index * block, 16)
        return pltpu.make_async_copy(
            table.at[pl.ds(start, block)], buf.at[slot], sems.at[slot]
        )

    first = pltpu.make_async_copy(table.at[pl.ds(blocks * block, tail_rows)], tail, sems.at[2])
    first.start()
    fetch(0, 0).start()
    rows[:half] = hm_ref[...]
    rows[half:] = ho_ref[...]
    first.wait()
    s = mm_nt(rows[...], tail[...])
    m = jnp.max(s, -1, keepdims=True)
    p = jnp.exp(s - m)
    peak[...] = jnp.broadcast_to(m, (count, 128))
    total[...] = jnp.broadcast_to(jnp.sum(p, -1, keepdims=True), (count, 128))
    acc[...] = mm(p.astype(bf16), tail[...])

    def body(index, _):
        slot = lax.rem(index, 2)

        @pl.when(index + 1 < blocks)
        def _():
            fetch(index + 1, 1 - slot).start()

        fetch(index, slot).wait()
        s = mm_nt(rows[...], buf[slot])
        m_old = peak[:, :1]
        m = jnp.maximum(m_old, jnp.max(s, -1, keepdims=True))
        decay = jnp.exp(m_old - m)
        p = jnp.exp(s - m)
        peak[...] = jnp.broadcast_to(m, (count, 128))
        total[...] = total[...] * decay + jnp.sum(p, -1, keepdims=True)
        acc[...] = acc[...] * decay + mm(p.astype(bf16), buf[slot])
        return 0

    lax.fori_loop(0, blocks, body, 0)
    column = lax.broadcasted_iota(jnp.int32, (count, 128), 1)
    stats = jnp.transpose(jnp.where(column == 0, peak[...], total[...]))
    own_stat[...] = stats[:8, :half]
    mine_ref[...] = acc[:half]
    theirs_ref[:half] = acc[half:].astype(bf16)
    theirs_ref[half:] = pack_stats(stats[:8, half:], theirs_ref.shape[1])


def head(hm, ho, table):
    half, width = hm.shape
    vocab = table.shape[0]
    block = min(VOCAB_BLOCK, vocab)
    tail_rows = vocab % block or block
    return pl.pallas_call(
        functools.partial(head_kernel, block),
        out_shape=(
            shape((half, width), f32), shape((half + 16, width), bf16), shape((8, half), f32),
        ),
        in_specs=[VM, VM, HBM],
        out_specs=(VM,) * 3,
        scratch_shapes=[
            pltpu.VMEM((2, block, width), bf16),
            pltpu.VMEM((tail_rows, width), bf16),
            pltpu.SemaphoreType.DMA((3,)),
            pltpu.VMEM((2 * half, 128), f32),
            pltpu.VMEM((2 * half, 128), f32),
            pltpu.VMEM((2 * half, width), bf16),
            pltpu.VMEM((2 * half, width), f32),
        ],
        compiler_params=pltpu.CompilerParams(vmem_limit_bytes=40 << 20),
        cost_estimate=pl.CostEstimate(
            flops=8 * half * vocab * width,
            bytes_accessed=2 * vocab * width,
            transcendentals=2 * half * vocab,
        ),
        name="vocabulary_head",
    )(hm, ho, table)


def stat_columns(stats):
    spread = jnp.transpose(jnp.concatenate([stats] * 16, 0))
    return spread[:, 0:1], spread[:, 1:2]


def merge_stats(own, got):
    own_peak, own_total = stat_columns(own)
    got_peak, got_total = stat_columns(got)
    peak = jnp.maximum(own_peak, got_peak)
    own_decay = jnp.exp(own_peak - peak)
    got_decay = jnp.exp(got_peak - peak)
    return peak, own_total * own_decay + got_total * got_decay, own_decay, got_decay


def merge_kernel(mine_ref, own_ref, got_ref, total_ref, stat_ref):
    count = own_ref.shape[1]
    peak, total, own_decay, got_decay = merge_stats(
        own_ref[...], unpack_stats(got_ref[count:, :], count)
    )
    total_ref[:count] = (
        mine_ref[:count].astype(f32) * own_decay + got_ref[:count].astype(f32) * got_decay
    ).astype(bf16)
    column = lax.broadcasted_iota(jnp.int32, (count, 128), 1)
    stats = jnp.transpose(jnp.where(column == 0, peak, total))[:8]
    stat_ref[...] = stats
    total_ref[count:] = pack_stats(stats, total_ref.shape[1])


def merge(mine, own_stat, got):
    return call(
        merge_kernel,
        [shape(got.shape, bf16), shape(own_stat.shape, f32)],
        [mine, own_stat, got],
        [VM] * 3,
        name="merge",
    )


def loss_back_kernel(
    place, weight_ref, total_ref, own_ref, got_ref, row_ref, row_got_ref,
    h_ref, x_ref, gain_ref, dx_out, low_out, loss_out,
):
    weight = weight_ref[0]
    count = own_ref.shape[1]
    peak, total, own_decay, got_decay = merge_stats(
        own_ref[...], unpack_stats(got_ref[count:, :], count)
    )
    log_total = peak + jnp.log(total)
    rows = row_ref[...].astype(f32) + row_got_ref[...].astype(f32)
    picked = jnp.sum(h_ref[...].astype(f32) * rows, -1, keepdims=True)
    loss = jnp.sum(log_total - picked, 0, keepdims=True)
    loss_out[...] = jnp.broadcast_to(loss * weight, loss_out.shape)
    wanted = weight * jnp.exp(picked - log_total)
    coefficient = (wanted - weight).astype(bf16).astype(f32) - wanted
    scale = weight / total
    grad = (
        total_ref[:count].astype(f32) * (own_decay * scale)
        + got_ref[:count].astype(f32) * (got_decay * scale)
        + coefficient * rows
    )
    dx = norm_derivative(grad, x_ref[...], gain_ref[place : place + 1, :])
    dx_out[...] = dx
    low_out[...] = dx.astype(bf16)


def loss_backward(weight, total, own_stat, got, row, row_got, h, x, gains):
    ins = [weight, total, own_stat, got, row, row_got, h, x, gains]
    return call(
        functools.partial(loss_back_kernel, 2),
        [shape(x.shape, f32), shape(x.shape, bf16), shape((8, 128), f32)],
        ins,
        [SM] + [VM] * 8,
        name="loss_backward",
    )


def mlp_back_kernel(
    dm_ref, do_ref, hm_ref, ho_ref, g_ref, slope_ref, ue_ref, uc_ref, we_ref, wc_ref,
    stack_ref, *refs
):
    mine_ref, theirs_ref, grad_ref = refs[-3:]
    hidden, width = wc_ref.shape
    starts = [0, width, 2 * width, 2 * width + hidden, 2 * width + 2 * hidden]
    starts += [2 * width + 3 * hidden, 3 * width + 3 * hidden]
    bch_ref, bcl_ref, acx_ref, beh_ref, bel_ref, aex_ref = (
        stack_ref.at[:, a:b] for a, b in zip(starts[:-1], starts[1:])
    )
    earlier = refs[:-3]
    for place, d_ref, h_ref in ((1, do_ref, ho_ref), (0, dm_ref, hm_ref)):
        d = d_ref[...]
        duc = split_columns(mm_nt(d, bch_ref[...]) + mm_nt(d, bcl_ref[...]), 4)
        dg = mm_nt(d, wc_ref[...]) + mm(duc, acx_ref[...])
        df = (dg * slope_ref[place]).astype(bf16)
        due = split_columns(mm_nt(df, beh_ref[...]) + mm_nt(df, bel_ref[...]), 4)
        part = mm_nt(df, we_ref[...]) + mm(due, aex_ref[...])
        grads = jnp.concatenate(
            [
                mm_tn(uc_ref[place], d), mm_tn(duc, g_ref[place]),
                mm_tn(ue_ref[place], df), mm_tn(due, h_ref[...]),
            ],
            1,
        )
        if place:
            theirs_ref[...] = part.astype(bf16)
            grad_ref[...] = grads + earlier[0][...] if earlier else grads
        else:
            mine_ref[...] = part
            grad_ref[...] += grads


def output_back_kernel(
    side_ref, dm_ref, do_ref, o_ref, u_ref, wo_ref, bh_ref, bl_ref, ax_ref, *refs
):
    grad_out, grad_ref = refs[-2:]
    earlier = refs[:-2]
    side = side_ref[0]
    for place, d_ref in enumerate((dm_ref, do_ref)):
        half = side if place == 0 else 1 - side
        d = d_ref[...]
        du = split_columns(mm_nt(d, bh_ref[...]) + mm_nt(d, bl_ref[...]), 4)
        grad_out[half] = (mm_nt(d, wo_ref[...]) + mm(du, ax_ref[...])).astype(bf16)
        grads = jnp.concatenate([mm_tn(u_ref[half], d), mm_tn(du, o_ref[half])], 1)
        if place:
            grad_ref[...] += grads
        else:
            grad_ref[...] = grads + earlier[0][...] if earlier else grads


def attention_back_kernel(place, heads, b_ref, grad_in, lse_ref, *refs):
    chunks = place + 1
    qkv_refs = refs[:chunks]
    h_refs = refs[chunks : 2 * chunks]
    u_refs = refs[2 * chunks : 3 * chunks]
    earlier = refs[3 * chunks : -5]
    gb_ref, ga_ref, kt, dqt, dqkv = refs[-5:]
    _, _, half_rows, width = qkv_refs[0].shape
    rows = 2 * half_rows
    for p in range(chunks):
        kt[:, p * rows : (p + 1) * rows] = jnp.transpose(
            qkv_refs[p][1].reshape(rows, width).astype(f32) * score_scale
        ).astype(bf16)
    dqkv[1:] = jnp.zeros((2,) + dqkv.shape[1:], f32)
    lane = lax.broadcasted_iota(jnp.int32, (half_rows, width), 1) // HEAD_DIM
    key = lax.broadcasted_iota(jnp.int32, (half_rows, half_rows), 0)
    query = lax.broadcasted_iota(jnp.int32, (half_rows, half_rows), 1)
    causal = key <= query
    for b in range(2):
        segments = [
            (p * rows, rows, qkv_refs[p][1].reshape(rows, width), qkv_refs[p][2].reshape(rows, width))
            for p in range(place)
        ]
        segments += [
            (place * rows + i * half_rows, half_rows, qkv_refs[place][1, i], qkv_refs[place][2, i])
            for i in range(b + 1)
        ]
        q = (qkv_refs[place][0, b].astype(f32) * score_scale).astype(bf16)
        grad = grad_in[b]
        for head in range(heads):
            q_head = jnp.where(lane == head, q, jnp.zeros_like(q))
            grad_head = jnp.where(lane == head, grad, jnp.zeros_like(grad))
            lse = lse_ref[head : head + 1, b * half_rows : (b + 1) * half_rows]
            weights = []
            products = []
            inner = None
            for i, (start, count, k, v) in enumerate(segments):
                s = mm_nt(k, q_head)
                if i == len(segments) - 1:
                    s = jnp.where(causal, s, -1e30)
                w = jnp.exp(s - lse)
                dw = mm_nt(v, grad_head)
                term = jnp.sum(w * dw, 0, keepdims=True)
                inner = term if inner is None else inner + term
                weights.append(w)
                products.append(dw)
            part = None
            for (start, count, k, v), w, dw in zip(segments, weights, products):
                ds = (w * (dw - inner)).astype(bf16)
                dqkv[1, start : start + count, :] += mm(ds, q_head)
                dqkv[2, start : start + count, :] += mm(w.astype(bf16), grad_head)
                term = mm(kt[head * HEAD_DIM : (head + 1) * HEAD_DIM, start : start + count], ds)
                part = term if part is None else part + term
            dqt[head * HEAD_DIM : (head + 1) * HEAD_DIM, :] = part
        start = place * rows + b * half_rows
        dqkv[0, start : start + half_rows, :] = jnp.transpose(dqt[...])
    if earlier:
        gb_ref[...] = earlier[0][...]
        ga_ref[...] = earlier[1][...]
    else:
        gb_ref[...] = jnp.zeros_like(gb_ref)
        ga_ref[...] = jnp.zeros_like(ga_ref)
    for p in range(chunks):
        for b in range(2):
            start = p * rows + b * half_rows
            u = u_refs[p][b]
            t = None
            for j in range(0 if p == place else 1, 3):
                d = dqkv[j, start : start + half_rows, :]
                high = d.astype(bf16)
                low = (d - high.astype(f32)).astype(bf16)
                gb_ref[j] += mm_tn(u, high) + mm_tn(u, low)
                term = mm_nt(high, b_ref[j]) + mm_nt(high, b_ref[3 + j]) + mm_nt(low, b_ref[j])
                t = term if t is None else t + term
            ga_ref[...] += mm_tn(split_columns(t, 12), h_refs[p][b])


def assemble_kernel(
    rank, side_ref, gb_ref, ga_ref, mlp_ref, out_ref, keep_ref, send_ref, own_ref
):
    width = ga_ref.shape[1]
    part = gb_ref.shape[2]
    hidden = (mlp_ref.shape[1] - 2 * width) // 2
    third = 3 * rank

    def folded(values):
        return values[:rank] + values[rank : 2 * rank]

    ga = ga_ref[:third, :] + ga_ref[third : 2 * third, :]
    mlp = mlp_ref[...]
    out = out_ref[...]
    first = jnp.concatenate([ga[rank * j : rank * (j + 1)] for j in range(3)], 1)
    second = jnp.concatenate(
        [
            folded(mlp[:, width + 2 * hidden :]),
            adapter_scale * folded(out[:, :width]),
            adapter_scale * folded(mlp[:, :width]),
        ],
        1,
    )

    @pl.when(side_ref[0] == 0)
    def _():
        keep_ref[...] = first
        send_ref[...] = second

    @pl.when(side_ref[0] != 0)
    def _():
        keep_ref[...] = second
        send_ref[...] = first

    pieces = []
    for j in range(3):
        gb = gb_ref[j, :third, :] + gb_ref[j, third : 2 * third, :]
        pieces.append(adapter_scale * gb[rank * j : rank * (j + 1)])
    pieces.append(folded(out[:, width:]))
    pieces.append(folded(mlp[:, width : width + hidden]))
    pieces.append(adapter_scale * folded(mlp[:, width + hidden : width + 2 * hidden]))
    own_ref[...] = jnp.concatenate(pieces, 1)


def adam_kernel(part, hidden, order, gathered_ref, *refs):
    weight_refs, first_refs, second_refs = (refs[4 * i : 4 * i + 4] for i in range(3))
    norm_ref = refs[12]
    outs = refs[13:]
    count = gathered_ref.shape[0]
    width = weight_refs[0].shape[2]
    piece = 6 * width // count
    shared = jnp.concatenate([gathered_ref[i, :, :piece] for i in range(count)], 1)
    shared = [shared[:, i * width : (i + 1) * width] for i in range(6)]

    def whole(start, size):
        start += piece
        return jnp.concatenate([gathered_ref[i, :, start : start + size] for i in order], 1)

    model_down = [*shared[:3], whole(3 * part, part), shared[3]]
    model_up = [*(whole(j * part, part) for j in range(3)), *shared[4:]]
    hidden_down = whole(4 * part, hidden)
    hidden_up = whole(4 * part + hidden, hidden)
    items = [(0, j, model_down[j]) for j in range(5)] + [(2, j, model_up[j]) for j in range(5)]
    items += [(1, None, hidden_down), (3, None, hidden_up)]
    squares = jnp.zeros((1, 1), f32)
    for _, _, value in items:
        squares = squares + jnp.sum(
            jnp.sum(value * value, 1, keepdims=True), 0, keepdims=True
        )
    norm = jnp.sqrt(squares)
    row = lax.broadcasted_iota(jnp.int32, norm_ref.shape, 0)
    losses = [gathered_ref[i, 0:1, gathered_ref.shape[2] - 128 :] for i in order[:2]]
    norm_ref[...] = jnp.where(row == 0, norm, losses[0] + losses[1])
    factor = clip_limit / jnp.maximum(norm, clip_limit)
    first_fix = 1.0 - beta_one**ADAM_STEP
    second_fix = 1.0 - beta_two**ADAM_STEP
    for place, j, value in items:
        at = ... if j is None else j
        grad = value * factor
        first = beta_one * first_refs[place][at] + (1.0 - beta_one) * grad
        second = beta_two * second_refs[place][at] + (1.0 - beta_two) * grad * grad
        stride = first / first_fix / (jnp.sqrt(second / second_fix) + adam_eps)
        weight = weight_refs[place][at]
        outs[place][at] = weight - learn_rate * (stride + decay_rate * weight)
        outs[4 + place][at] = first
        outs[8 + place][at] = second


def adam(part, hidden, order, gathered, weights, firsts, seconds):
    shapes = [shape(w.shape, f32) for w in weights]
    ins = [gathered, *weights, *firsts, *seconds]
    return call(
        functools.partial(adam_kernel, part, hidden, order),
        [shape((8, 128), f32)] + shapes * 3,
        ins,
        [VM] * 13,
        name="adam",
    )


def prepare_kernel(
    index_ref, down_ref, hidden_down_ref, up_ref, hidden_up_ref,
    a_attention, b_attention, b_attention_back,
    a_output, a_expand, a_contract,
    b_output, b_output_high, b_output_low,
    b_contract, b_expand, twice_output, mlp_back,
):
    rank = down_ref.shape[1]
    width = down_ref.shape[2]
    part = a_output.shape[1]
    hidden = a_contract.shape[1]
    own = pl.ds(pl.multiple_of(index_ref[0] * part, 128), part)
    own_hidden = pl.ds(pl.multiple_of(index_ref[0] * hidden, 128), hidden)

    def put(ref, pieces):
        rows = jnp.concatenate(pieces, 0)
        missing = ref.shape[0] - rows.shape[0]
        if missing:
            rows = jnp.concatenate([rows, jnp.zeros((missing, rows.shape[1]), f32)], 0)
        ref[...] = rows.astype(bf16)

    def parts(values):
        high = values.astype(bf16).astype(f32)
        return high, values - high

    starts = [0, width, 2 * width, 2 * width + hidden, 2 * width + 2 * hidden]
    starts += [2 * width + 3 * hidden, 3 * width + 3 * hidden]
    (
        b_contract_high, b_contract_low, twice_contract, b_expand_high, b_expand_low, twice_expand,
    ) = (mlp_back.at[:, a:b] for a, b in zip(starts[:-1], starts[1:]))
    put(a_attention, [down_ref[j] for j in range(3)] * 3)
    for values, three, two in (
        (down_ref[3, :, own], a_output, twice_output),
        (down_ref[4], a_expand, twice_expand),
        (hidden_down_ref[:, own_hidden], a_contract, twice_contract),
    ):
        put(three, [values] * 3)
        put(two, [values] * 2)
    for values, both, high_ref, low_ref in (
        (up_ref[3], b_output, b_output_high, b_output_low),
        (up_ref[4], b_contract, b_contract_high, b_contract_low),
        (hidden_up_ref[:, own_hidden], b_expand, b_expand_high, b_expand_low),
    ):
        high, low = parts(adapter_scale * values)
        put(both, [high, high, low])
        put(high_ref, [high] * 3)
        put(low_ref, [low] * 3)
    zero = jnp.zeros((rank, part), f32)
    for j in range(3):
        high, low = parts(adapter_scale * up_ref[j, :, own])
        placed_high = [high if i == j else zero for i in range(3)]
        placed_low = [low if i == j else zero for i in range(3)]
        put(b_attention.at[j], placed_high * 2 + placed_low)
        put(b_attention_back.at[j], placed_high * 3)
        put(b_attention_back.at[3 + j], placed_low * 3)


def prepare(index, down, hidden_down, up, hidden_up, part, hidden):
    width = down.shape[2]
    rank = down.shape[1]
    wide = 9 * rank + -9 * rank % 16
    thin = 3 * rank + -3 * rank % 16
    attention = [shape((3, wide, part), bf16), shape((6, wide, part), bf16)]
    a_shapes = [shape((thin, n), bf16) for n in (part, width, hidden)]
    b_shapes = [shape((thin, n), bf16) for n in (width, width, width, width, hidden, part)]
    packed = shape((thin, 3 * width + 3 * hidden), bf16)
    return call(
        prepare_kernel,
        [shape((wide, width), bf16), *attention, *a_shapes, *b_shapes, packed],
        [index, down, hidden_down, up, hidden_up],
        [SM] + [VM] * 4,
        name="prepare",
        room=6,
    )


def shards(
    tensor_size,
    batch_size,
    token_ids,
    targets,
    task_groups,
    embedding,
    positions,
    norm_gains,
    norm_shifts,
    w_qkv,
    attention_output_weight,
    expand_weight,
    contract_weight,
    model_down_maps,
    hidden_down_map,
    model_up_maps,
    hidden_up_map,
    model_down_first,
    hidden_down_first,
    model_up_first,
    hidden_up_first,
    model_down_second,
    hidden_down_second,
    model_up_second,
    hidden_up_second,
):
    assert token_ids.shape[0] == 1
    assert tensor_size >= 4 and tensor_size & (tensor_size - 1) == 0
    assert batch_size & (batch_size - 1) == 0
    index = lax.axis_index("tensor")
    side = index % 2
    length = token_ids.shape[1]
    vocab, width = embedding.shape
    part = attention_output_weight.shape[0]
    hidden = expand_weight.shape[1]
    rank = model_down_maps.shape[2]
    heads = part // HEAD_DIM
    half = length // (2 * CHUNKS)
    side_arg = side.astype(jnp.int32).reshape(1)
    steps = []
    bit = 1
    while bit < tensor_size:
        steps.append(bit)
        bit *= 2

    def swap(value, step, axis="tensor"):
        size = tensor_size if axis == "tensor" else batch_size
        return lax.ppermute(value, axis, [(i, i ^ step) for i in range(size)])

    def pick(value, which):
        return lax.dynamic_index_in_dim(value, which, 0, keepdims=False)

    def after(value, *others):
        return lax.optimization_barrier((value, *others))[0]

    def reduce_rows(mine, theirs):
        total = (mine.astype(f32) + swap(theirs, 1).astype(f32)).astype(bf16)
        for step in steps[1:-1]:
            total = (total.astype(f32) + swap(total, step).astype(f32)).astype(bf16)
        return total, swap(total, steps[-1])

    gather_place = jnp.stack([side, index * vocab]).astype(jnp.int32)

    def lookup(ids):
        rows = gather(gather_place, ids.reshape(-1), embedding, half)
        return [rows[2 * n : 2 * n + 2] for n in range(CHUNKS)]

    down = jnp.swapaxes(model_down_maps, 1, 2)
    hidden_down = jnp.swapaxes(hidden_down_map, 0, 1)
    (
        a_attention, b_attention, b_attention_back,
        a_output, a_expand, a_contract,
        b_output, b_output_high, b_output_low,
        b_contract, b_expand, twice_output, mlp_back_stack,
    ) = prepare(
        index.astype(jnp.int32).reshape(1), down, hidden_down, model_up_maps, hidden_up_map,
        part, hidden,
    )
    wide_rows = a_attention.shape[0]
    thin_rows = a_output.shape[0]

    position_halves = positions.reshape(CHUNKS, 2, half, width)
    wqkv = jnp.transpose(w_qkv, (1, 0, 2))
    member = (task_groups[:, None] == jnp.arange(GROUPS)[None, :]).astype(jnp.int32)
    counts = [jnp.sum(member, 0) * length]

    def count_step(value):
        step = 2 ** (len(counts) - 1)
        if step >= batch_size:
            return value
        counts.append(counts[-1] + swap(counts[-1], step, "batch"))
        return after(value, counts[-1])

    embedded = [reduce_rows(*rows) for rows in lookup(token_ids)]
    wanted_rows = lookup(after(targets, *(pair[0] for pair in embedded)))
    held = lax.optimization_barrier(
        (count_step(embedded[0][0]), *(row for pair in wanted_rows for row in pair))
    )
    embedded[0] = (held[0], embedded[0][1])
    wanted_rows = [held[1 + 2 * n : 3 + 2 * n] for n in range(CHUNKS)]
    x0, qkv, h1, u1, normed = [], [], [], [], []
    for n in range(CHUNKS):
        x, h = norm_forward(
            0, *embedded[n], pick(position_halves[n], side), norm_gains, norm_shifts
        )
        x0.append(x)
        normed.append((h, swap(h, 1)))
    for n in range(CHUNKS):
        own, other = normed[n]
        if n == 0:
            own = after(own, normed[-1][0])
        one = call(
            qkv_kernel,
            [
                shape((3, 2, half, part), bf16),
                shape((2, half, width), bf16),
                shape((2, half, wide_rows), bf16),
            ],
            [side_arg, count_step(own) if n else own, other, wqkv, a_attention, b_attention],
            [SM] + [VM] * 5,
            flops=2 * 2 * half * width * 4 * part,
            name="qkv",
        )
        qkv.append(one[0])
        h1.append(one[1])
        u1.append(one[2])

    o, lse, uo, x1, h2, reduced = [], [], [], [], [], []
    for n in range(CHUNKS):
        current = qkv[: n + 1]
        if n:
            current[-1] = after(current[-1], reduced[-1][0])
        mine, theirs, o_n, lse_n, u_n = call(
            functools.partial(attention_kernel, n, heads),
            [
                shape((half, width), f32),
                shape((half, width), bf16),
                shape((2, half, part), bf16),
                shape((8, 2 * half), f32),
                shape((2, half, thin_rows), bf16),
            ],
            [side_arg, attention_output_weight, a_output, b_output] + current,
            [SM] + [VM] * (4 + n),
            scratch=[
                pltpu.VMEM((part, (n + 1) * 2 * half), bf16),
                pltpu.VMEM((part, half), f32),
            ],
            flops=2 * 2 * half * (2 * n + 1.5) * half * part * heads + 4 * half * part * width,
            name=f"attention_{n}",
        )
        o.append(o_n)
        lse.append(lse_n)
        uo.append(u_n)
        reduced.append(reduce_rows(mine, theirs))
    for n in range(CHUNKS):
        x, h = norm_forward(1, *reduced[n], x0[n], norm_gains, norm_shifts)
        x1.append(x)
        h2.append((h, swap(h, 1)))

    saved, x2, hf, reduced = [], [], [], []
    for n in range(CHUNKS):
        own, other = h2[n]
        if n:
            own = after(own, reduced[-1][0])
            while 2 ** (len(counts) - 1) < batch_size:
                own = count_step(own)
        mine, theirs, *rest = call(
            mlp_kernel,
            [
                shape((half, width), f32),
                shape((half, width), bf16),
                shape((2, half, hidden), bf16),
                shape((2, half, hidden), f32),
                shape((2, half, thin_rows), bf16),
                shape((2, half, thin_rows), bf16),
            ],
            [
                own, other, expand_weight, contract_weight, a_expand, b_expand, a_contract,
                b_contract,
            ],
            [VM] * 8,
            flops=2 * 2 * half * width * hidden * 2,
            name="mlp",
        )
        saved.append(rest)
        reduced.append(reduce_rows(mine, theirs))

    def final_norm(n, total):
        x, h = norm_forward(2, total, reduced[n][1], x1[n], norm_gains, norm_shifts)
        x2.append(x)
        hf.append((h, swap(h, 1)))

    final_norm(0, reduced[0][0])

    seq_weight = (
        jnp.sum(jnp.where(member > 0, 1.0 / counts[-1].astype(f32)[None, :], 0.0), 1) / GROUPS
    )[0]
    weight_arg = seq_weight.reshape(1)
    ahead = after(hf[0][0], weight_arg)
    wanted_rows = [
        reduce_rows(after(rows[0], ahead), after(rows[1], ahead)) for rows in wanted_rows
    ]
    parts = []
    for n in range(CHUNKS):
        if n:
            final_norm(n, after(reduced[n][0], theirs))
        own, other = hf[n]
        own = after(own, *(parts[-1][:1] if n else [pair[0] for pair in wanted_rows]))
        mine, theirs, own_stat = head(own, other, embedding)
        if n == 0:
            theirs = after(theirs, *(row for pair in wanted_rows for row in pair))
        total, stat = merge(mine, own_stat, swap(theirs, 1))
        for step in steps[1:-1]:
            total, stat = merge(total, stat, swap(total, step))
        parts.append((total, stat, swap(total, steps[-1])))
    losses, dx2, dm = [], [], []
    for n in range(CHUNKS):
        dx, low, loss_n = loss_backward(
            weight_arg, *parts[n], *wanted_rows[n], hf[n][0], x2[n], norm_gains
        )
        dx2.append(dx)
        dm.append((low, swap(low, 1)))
        losses.append(loss_n)
    loss = functools.reduce(jnp.add, losses)

    dx1, grads_mlp, reduced = [], [], []

    def middle(n):
        _, low = norm_backward(1, *reduced[n], x1[n], norm_gains, dx2[n])
        dx1.append((low, swap(low, 1)))
        return low

    for n in range(CHUNKS):
        g, slope, ue, uc = saved[n]
        own, other = dm[n]
        own = after(own, reduced[-1][0] if n else parts[-1][0])
        mine, theirs, grads = call(
            mlp_back_kernel,
            [
                shape((half, width), f32),
                shape((half, width), bf16),
                shape((thin_rows, 2 * width + 2 * hidden), f32),
            ],
            [
                own, other, *h2[n], g, slope, ue, uc, expand_weight, contract_weight,
                mlp_back_stack, *grads_mlp[-1:],
            ],
            [VM] * (12 if n else 11),
            flops=2 * 2 * half * width * hidden * 2,
            name="mlp_back",
        )
        grads_mlp.append(grads)
        if n:
            mine = after(mine, middle(n - 1))
        reduced.append(reduce_rows(mine, theirs))

    grads_output, grads_attention = [], []
    for n in range(CHUNKS):
        if n == CHUNKS - 1:
            if n:
                reduced[n] = (after(reduced[n][0], grads_attention[0]), reduced[n][1])
            middle(n)
        grad_n, grads = call(
            output_back_kernel,
            [shape((2, half, part), bf16), shape((thin_rows, width + part), f32)],
            [
                side_arg, *dx1[n], o[n], uo[n], attention_output_weight,
                b_output_high, b_output_low, twice_output, *grads_output[-1:],
            ],
            [SM] + [VM] * (9 if n else 8),
            flops=4 * half * width * part * 2,
            name="output_back",
        )
        grads_output.append(grads)
        grads_attention = call(
            functools.partial(attention_back_kernel, n, heads),
            [shape((3, wide_rows, part), f32), shape((wide_rows, width), f32)],
            [
                b_attention_back, grad_n, lse[n],
                *qkv[: n + 1], *h1[: n + 1], *u1[: n + 1], *grads_attention,
            ],
            [VM] * (3 + 3 * (n + 1) + len(grads_attention)),
            scratch=[
                pltpu.VMEM((part, (n + 1) * 2 * half), bf16),
                pltpu.VMEM((part, half), f32),
                pltpu.VMEM((3, (n + 1) * 2 * half, part), f32),
            ],
            flops=5 * (n + 1) * length * half * part * heads,
            name=f"attention_back_{n}",
        )
    keep, send, own = call(
        functools.partial(assemble_kernel, rank),
        [shape((rank, 3 * width), f32)] * 2 + [shape((rank, 4 * part + 2 * hidden), f32)],
        [side_arg, *grads_attention, grads_mlp[-1], grads_output[-1]],
        [SM] + [VM] * 4,
        name="assemble",
    )

    bits = [(index // step) % 2 for step in steps]
    shared = keep + swap(send, steps[0])
    for step, bit in zip(steps[1:], bits[1:]):
        columns = shared.shape[1] // 2
        keep = lax.dynamic_slice_in_dim(shared, bit * columns, columns, 1)
        send = lax.dynamic_slice_in_dim(shared, (1 - bit) * columns, columns, 1)
        shared = keep + swap(send, step)
    loss_column = loss[:rank]
    bundle = jnp.concatenate([shared, own, loss_column], 1)
    step = 1
    while step < batch_size:
        bundle = bundle + swap(bundle, step, "batch")
        step *= 2
    gathered = bundle[None]
    for step, bit in reversed(list(zip(steps, bits))):
        other = swap(gathered, step)
        gathered = jnp.where(
            bit == 0,
            jnp.concatenate([gathered, other], 0),
            jnp.concatenate([other, gathered], 0),
        )
    order = []
    for place in range(tensor_size):
        slot = 0
        for i in range(len(steps)):
            slot = slot * 2 + (place >> i) % 2
        order.append(slot)
    def turned(values):
        return [
            jnp.swapaxes(values[0], 1, 2), jnp.swapaxes(values[1], 0, 1), values[2], values[3],
        ]

    weights = (model_down_maps, hidden_down_map, model_up_maps, hidden_up_map)
    firsts = (model_down_first, hidden_down_first, model_up_first, hidden_up_first)
    seconds = (model_down_second, hidden_down_second, model_up_second, hidden_up_second)
    norm, *news = adam(
        part,
        hidden,
        order,
        gathered,
        turned(weights),
        turned(firsts),
        turned(seconds),
    )
    return (norm[1, 0], norm[0, 0], *turned(news[:4]), *turned(news[4:8]), *turned(news[8:]))


def solution(mesh):
    none = P()
    return jax.shard_map(
        functools.partial(shards, mesh.shape["tensor"], mesh.shape["batch"]),
        mesh=mesh,
        in_specs=(
            P("batch", None),
            P("batch", None),
            P("batch"),
            P("tensor", None),
            none,
            none,
            none,
            P(None, None, "tensor"),
            P("tensor", None),
            P(None, "tensor"),
            P("tensor", None),
        )
        + (none,) * 12,
        out_specs=(none,) * 14,
        check_vma=False,
    )
```

profile of v0, /device:TPU:0, one launch (start us, length us, event | category | flops | bytes accessed | tf_op | source)
XLA Modules:
  0.0 286.9 jit_solution(16860387262003189077)
XLA Ops:
  1.4 11.3 %gather.2 = (bf16[256,1024]{1,0:T(8,128)(2,1)S(1)}, bf16[256,1024]{1,0:T(8,128)(2,1)S(1)}, bf16[256,1024]{1,0:T(8,128)(2,1)S(1)}, bf16[256,1024]{1,0:T(8,128)(2,1)S(1)}) custom-call(s32[2]{0:T(128)S(1)} %pad_add_fusion.place_ref, s32[1024]{0:T(1024)S(1)} %bitcast.42, bf16[12576,1024]{1,0:T(8,128)(2,1)} %table.7), custom_call_target="tpu_custom_call" | custom-call | flops 1 | bytes 16777216 | tf_op jit(solution)/shard_map/gather/pallas_call | solution.py:139
  12.7 0.8 collective-permute-start.3
  14.2 2.4 collective-permute-start
  16.8 1.7 fusion.3
  19.3 1.2 add_convert_fusion.9.sum_ref
  20.5 1.8 collective-permute-start.5
  23.0 11.3 %gather.3 = (bf16[256,1024]{1,0:T(8,128)(2,1)S(1)}, bf16[256,1024]{1,0:T(8,128)(2,1)S(1)}, bf16[256,1024]{1,0:T(8,128)(2,1)S(1)}, bf16[256,1024]{1,0:T(8,128)(2,1)S(1)}) custom-call(s32[2]{0:T(128)S(1)} %pad_add_fusion.place_ref, s32[1024]{0:T(1024)S(1)} %bitcast.43, bf16[12576,1024]{1,0:T(8,128)(2,1)} %table.7), custom_call_target="tpu_custom_call" | custom-call | flops 1 | bytes 16777216 | tf_op jit(solution)/shard_map/gather/pallas_call | solution.py:139
  38.0 8.0 %collective-permute-done.6.got_ref = bf16[256,1024]{1,0:T(8,128)(2,1)S(1)} collective-permute-done((bf16[256,1024]{1,0:T(8,128)(2,1)S(1)}, bf16[256,1024]{1,0:T(8,128)(2,1)S(1)}, u32[]{:S(2)}, u32[]{:S(2)}) %collective-permute-start.6) | collective-permute-done | bytes 524320 | tf_op jit(solution)/shard_map/ppermute | solution.py:842
  46.6 1.8 qkv.2
  48.4 3.8 %attention_0.1 = (f32[256,1024]{1,0:T(8,128)S(1)}, bf16[256,1024]{1,0:T(8,128)(2,1)S(1)}, bf16[2,256,256]{2,1,0:T(8,128)(2,1)S(1)}, f32[8,512]{1,0:T(8,128)S(1)}, bf16[2,256,16]{2,1,0:T(8,128)(2,1)S(1)}) custom-call(s32[1]{0:T(128)} %bitcast.side_ref, bf16[256,1024]{1,0:T(8,128)(2,1)S(1)} %copy-done.10, bf16[16,256]{1,0:T(8,128)(2,1)S(1)} %get-tuple-element.149.a_ref, ...), custom_call_target="tpu_custom_call" | custom-call | flops 671088640 | bytes 3219460 | tf_op jit(solution)/shard_map/attention_0/pallas_call | solution.py:51
  52.8 1.7 collective-permute-start.1
  54.7 1.8 collective-permute-start.12
  56.5 1.8 qkv.3
  58.4 0.9 copy-done.76
  59.3 6.3 %attention_1.1 = (f32[256,1024]{1,0:T(8,128)S(1)}, bf16[256,1024]{1,0:T(8,128)(2,1)S(1)}, bf16[2,256,256]{2,1,0:T(8,128)(2,1)S(1)}, f32[8,512]{1,0:T(8,128)S(1)}, bf16[2,256,16]{2,1,0:T(8,128)(2,1)S(1)}) custom-call(s32[1]{0:T(128)} %bitcast.side_ref, bf16[256,1024]{1,0:T(8,128)(2,1)S(1)} %copy-done.10, bf16[16,256]{1,0:T(8,128)(2,1)S(1)} %get-tuple-element.149.a_ref, ...), custom_call_target="tpu_custom_call" | custom-call | flops 1207959552 | bytes 4005892 | tf_op jit(solution)/shard_map/attention_1/pallas_call | solution.py:51
  65.7 2.7 collective-permute-done.12.got_ref
  68.9 1.0 copy-done.3
  70.1 1.8 collective-permute-start.11
  71.9 5.7 %mlp.2 = (f32[256,1024]{1,0:T(8,128)S(1)}, bf16[256,1024]{1,0:T(8,128)(2,1)S(1)}, bf16[2,256,1024]{2,1,0:T(8,128)(2,1)S(1)}, f32[2,256,1024]{2,1,0:T(8,128)S(1)}...) custom-call(bf16[256,1024]{1,0:T(8,128)(2,1)S(1)} %get-tuple-element.178.hm_ref, ...), custom_call_target="tpu_custom_call" | custom-call | flops 2147483648 | bytes 10125312 | tf_op jit(solution)/shard_map/mlp/pallas_call | solution.py:51
  78.0 6.5 %collective-permute-done.11.got_ref = bf16[256,1024]{1,0:T(8,128)(2,1)S(1)} collective-permute-done((bf16[256,1024]{1,0:T(8,128)(2,1)S(1)}, bf16[256,1024]{1,0:T(8,128)(2,1)S(1)}, u32[]{:S(2)}, u32[]{:S(2)}) %collective-permute-start.11) | collective-permute-done | bytes 524320 | tf_op jit(solution)/shard_map/ppermute | solution.py:842
  85.1 2.9 collective-permute-start.2
  87.9 1.0 add_convert_fusion.5.sum_ref
  88.9 1.8 collective-permute-start.17
  91.3 6.3 %mlp.3 = (f32[256,1024]{1,0:T(8,128)S(1)}, bf16[256,1024]{1,0:T(8,128)(2,1)}, bf16[2,256,1024]{2,1,0:T(8,128)(2,1)S(1)}, f32[2,256,1024]{2,1,0:T(8,128)S(1)}, bf...) custom-call(bf16[256,1024]{1,0:T(8,128)(2,1)S(1)} %get-tuple-element.186.hm_ref, ...), custom_call_target="tpu_custom_call" | custom-call | flops 2147483648 | bytes 10125312 | tf_op jit(solution)/shard_map/mlp/pallas_call | solution.py:51
  97.6 1.4 copy-done.6
  99.0 1.0 copy-done.13
  100.0 1.0 copy-done.17
  103.3 1.2 copy-done.4
  104.5 1.8 norm_forward_2.2
  107.1 1.2 add_convert_fusion.4.sum_ref
  108.3 1.7 collective-permute-start.23
  110.9 1.7 collective-permute-start.22
  112.5 44.1 %vocabulary_head.2 = (f32[256,1024]{1,0:T(8,128)S(1)}, bf16[272,1024]{1,0:T(8,128)(2,1)S(1)}, f32[8,256]{1,0:T(8,128)S(1)}) custom-call(bf16[256,1024]{1,0:T(8,128)(2,1)S(1)} %get-tuple-element.200.hm_ref.h_ref, bf16[256,1024]{1,0:T(8,128)(2,1)S(1)} %collective-permute-done.20.ho_ref, bf16[12576,1024]{1,0:T(8,128)(2,1)} %table.7), custom_call_target="tpu_custom_call" | custom-call | flops 26373783552 | bytes 25755648 | tf_op jit(solution)/shard_map/vocabulary_head/pallas_call | solution.py:387
  157.8 0.9 collective-permute-done.24.got_ref
  159.6 34.5 %vocabulary_head.3 = (f32[256,1024]{1,0:T(8,128)S(1)}, bf16[272,1024]{1,0:T(8,128)(2,1)S(1)}, f32[8,256]{1,0:T(8,128)S(1)}) custom-call(bf16[256,1024]{1,0:T(8,128)(2,1)S(1)} %get-tuple-element.209.hm_ref.h_ref, bf16[256,1024]{1,0:T(8,128)(2,1)S(1)} %collective-permute-done.25.ho_ref, bf16[12576,1024]{1,0:T(8,128)(2,1)} %table.7), custom_call_target="tpu_custom_call" | custom-call | flops 26373783552 | bytes 25755648 | tf_op jit(solution)/shard_map/vocabulary_head/pallas_call | solution.py:387
  194.2 1.4 loss_backward.3
  196.7 1.6 collective-permute-start.27
  198.4 6.2 %mlp_back.2 = (f32[256,1024]{1,0:T(8,128)S(1)}, bf16[256,1024]{1,0:T(8,128)(2,1)S(1)}, f32[16,4096]{1,0:T(8,128)S(1)}) custom-call(bf16[256,1024]{1,0:T(8,128)(2,1)S(1)} %get-tuple-element.220.dm_ref, bf16[256,1024]{1,0:T(8,128)(2,1)S(1)} %collective-permute-done.29.do_ref, bf16[256,1024]{1,0:T(8,128)(2,1)S(1)} %copy-done.29, ...), custom_call_target="tpu_custom_call" | custom-call | flops 2147483648 | bytes 11501568 | tf_op jit(solution)/shard_map/mlp_back/pallas_call | solution.py:51
  204.7 6.6 %collective-permute-done.27.got_ref = bf16[272,1024]{1,0:T(8,128)(2,1)S(1)} collective-permute-done((bf16[272,1024]{1,0:T(8,128)(2,1)S(1)}, bf16[272,1024]{1,0:T(8,128)(2,1)S(1)}, u32[]{:S(2)}, u32[]{:S(2)}) %collective-permute-start.27) | collective-permute-done | bytes 557088 | tf_op jit(solution)/shard_map/ppermute | solution.py:842
  211.4 1.4 loss_backward.2
  213.0 1.7 collective-permute-start.32
  214.8 6.4 %mlp_back.3 = (f32[256,1024]{1,0:T(8,128)S(1)}, bf16[256,1024]{1,0:T(8,128)(2,1)S(1)}, f32[16,4096]{1,0:T(8,128)S(1)}) custom-call(bf16[256,1024]{1,0:T(8,128)(2,1)S(1)} %get-tuple-element.228.dm_ref, bf16[256,1024]{1,0:T(8,128)(2,1)S(1)} %collective-permute-done.31.do_ref, bf16[256,1024]{1,0:T(8,128)(2,1)S(1)} %copy-done.21, ...), custom_call_target="tpu_custom_call" | custom-call | flops 2147483648 | bytes 11763712 | tf_op jit(solution)/shard_map/mlp_back/pallas_call | solution.py:51
  221.4 6.0 %collective-permute-done.32.got_ref = bf16[256,1024]{1,0:T(8,128)(2,1)S(1)} collective-permute-done((bf16[256,1024]{1,0:T(8,128)(2,1)S(1)}, bf16[256,1024]{1,0:T(8,128)(2,1)S(1)}, u32[]{:S(2)}, u32[]{:S(2)}) %collective-permute-start.32) | collective-permute-done | bytes 524320 | tf_op jit(solution)/shard_map/ppermute | solution.py:842
  227.4 1.7 norm_backward_1.2
  229.4 1.7 collective-permute-start.35
  231.2 2.0 output_back.2
  233.2 5.5 %attention_back_0.1 = (f32[3,48,256]{2,1,0:T(8,128)S(1)}, f32[48,1024]{1,0:T(8,128)S(1)}) custom-call(bf16[6,48,256]{2,1,0:T(8,128)(2,1)S(1)} %copy-done.73, bf16[2,256,256]{2,1,0:T(8,128)(2,1)S(1)} %get-tuple-element.244.grad_in, f32[8,512]{1,0:T(8,128)S(1)} %copy-done.87, bf16[3,2,256,256]{3,2,1,0:T(8,128)(2,1)S(1)} %copy-done.79, ...), custom_call_target="tpu_custom_call" | custom-call | flops 1342177280 | bytes 2654208 | tf_op jit(solution)/shard_map/attention_back_0/pallas_call | solution.py:51
  238.7 5.1 %collective-permute-done.35.got_ref = bf16[256,1024]{1,0:T(8,128)(2,1)S(1)} collective-permute-done((bf16[256,1024]{1,0:T(8,128)(2,1)S(1)}, bf16[256,1024]{1,0:T(8,128)(2,1)S(1)}, u32[]{:S(2)}, u32[]{:S(2)}) %collective-permute-start.35) | collective-permute-done | bytes 524320 | tf_op jit(solution)/shard_map/ppermute | solution.py:842
  243.8 1.7 norm_backward_1.3
  245.6 1.9 collective-permute-done.36.do_ref
  247.5 2.0 output_back.3
  249.5 9.6 %attention_back_1.1 = (f32[3,48,256]{2,1,0:T(8,128)S(1)}, f32[48,1024]{1,0:T(8,128)S(1)}) custom-call(bf16[6,48,256]{2,1,0:T(8,128)(2,1)S(1)} %copy-done.73, bf16[2,256,256]{2,1,0:T(8,128)(2,1)S(1)} %get-tuple-element.255.grad_in, f32[8,512]{1,0:T(8,128)S(1)} %copy-done.89, bf16[3,2,256,256]{3,2,1,0:T(8,128)(2,1)S(1)} %copy-done.79, ...), custom_call_target="tpu_custom_call" | custom-call | flops 2684354560 | bytes 4882432 | tf_op jit(solution)/shard_map/attention_back_1/pallas_call | solution.py:51
  259.4 1.1 collective-permute-done.37
  260.6 1.7 collective-permute-start.38
  262.2 2.2 collective-permute-done.38
  265.0 3.9 %collective-permute-done.39 = f32[4,4736]{1,0:T(4,128)S(1)} collective-permute-done((f32[4,4736]{1,0:T(4,128)S(1)}, f32[4,4736]{1,0:T(4,128)S(1)}, u32[]{:S(2)}, u32[]{:S(2)}) %collective-permute-start.39) | collective-permute-done | bytes 75808 | tf_op jit(solution)/shard_map/ppermute | solution.py:842
  269.0 1.7 collective-permute-start.40
  270.7 2.8 collective-permute-done.40
  273.4 1.8 collective-permute-start.41
  275.2 3.5 %collective-permute-done.41 = f32[4,4736]{1,0:T(4,128)S(1)} collective-permute-done((f32[4,4736]{1,0:T(4,128)S(1)}, f32[4,4736]{1,0:T(4,128)S(1)}, u32[]{:S(2)}, u32[]{:S(2)}) %collective-permute-start.41) | collective-permute-done | bytes 75808 | tf_op jit(solution)/shard_map/ppermute | solution.py:842
  278.8 1.7 collective-permute-start.42
  280.5 2.8 collective-permute-done.42
  283.4 1.4 collective-permute-done.43
  284.9 1.2 adam.1
  (267 shorter events, 18.7 us)
Async XLA Ops:
  12.7 5.8 %collective-permute-start.3 = (bf16[256,1024]{1,0:T(8,128)(2,1)S(1)}, bf16[256,1024]{1,0:T(8,128)(2,1)S(1)}, u32[]{:S(2)}, u32[]{:S(2)}) collective-permute-start(bf16[256,1024]{1,0:T(8,128)(2,1)S(1)} %get-tuple-element.152), channel_id=1, source_target_pairs={{0,1},{1,0},{2,3},{3,2},{4,5},{5,4},{6,7},{7,6},{8,9},{9,8},{10,11... | collective-permute-start | bytes 1572872 | tf_op jit(solution)/shard_map/ppermute | solution.py:842
  14.2 8.2 %collective-permute-start = (s32[4]{0:T(128)S(1)}, s32[4]{0:T(128)S(1)}, u32[]{:S(2)}, u32[]{:S(2)}) collective-permute-start(s32[4]{0:T(128)S(1)} %compare_select_fusion.1), channel_id=1, source_target_pairs={{0,4},{4,0},{8,12},{12,8},{16,20},{20,16},{24,28},{28,24},{1,5},{5... | collective-permute-start | bytes 56 | tf_op jit(solution)/shard_map/ppermute | solution.py:842
  16.6 5.8 %collective-permute-start.4 = (bf16[256,1024]{1,0:T(8,128)(2,1)S(1)}, bf16[256,1024]{1,0:T(8,128)(2,1)S(1)}, u32[]{:S(2)}, u32[]{:S(2)}) collective-permute-start(bf16[256,1024]{1,0:T(8,128)(2,1)S(1)} %get-tuple-element.155), channel_id=1, source_target_pairs={{0,1},{1,0},{2,3},{3,2},{4,5},{5,4},{6,7},{7,6},{8,9},{9,8},{10,11... | collective-permute-start | bytes 1572872 | tf_op jit(solution)/shard_map/ppermute | solution.py:842
  20.5 14.9 %collective-permute-start.5 = (bf16[256,1024]{1,0:T(8,128)(2,1)S(1)}, bf16[256,1024]{1,0:T(8,128)(2,1)S(1)}, u32[]{:S(2)}, u32[]{:S(2)}) collective-permute-start(bf16[256,1024]{1,0:T(8,128)(2,1)S(1)} %add_convert_fusion.9.sum_ref), channel_id=1, source_target_pairs={{0,2},{1,3},{2,0},{3,1},{4,6},{5,7},{6,4},{7,5},{8,10},{9,11},{10,... | collective-permute-start | bytes 1572872 | tf_op jit(solution)/shard_map/ppermute | solution.py:842
  22.6 23.5 %collective-permute-start.6 = (bf16[256,1024]{1,0:T(8,128)(2,1)S(1)}, bf16[256,1024]{1,0:T(8,128)(2,1)S(1)}, u32[]{:S(2)}, u32[]{:S(2)}) collective-permute-start(bf16[256,1024]{1,0:T(8,128)(2,1)S(1)} %add_convert_fusion.8.sum_ref), channel_id=1, source_target_pairs={{0,2},{1,3},{2,0},{3,1},{4,6},{5,7},{6,4},{7,5},{8,10},{9,11},{10,... | collective-permute-start | bytes 1572872 | tf_op jit(solution)/shard_map/ppermute | solution.py:842
  23.0 12.4 %copy-start.19 = (f32[3,1024]{1,0:T(4,128)S(1)}, f32[3,1024]{1,0:T(4,128)}, u32[]{:S(2)}) copy-start(f32[3,1024]{1,0:T(4,128)} %shift_ref.11) | copy-start | bytes 36868
  23.0 13.0 %copy-start.32 = (f32[5,1024,4]{1,2,0:T(4,128)S(1)}, f32[5,1024,4]{1,2,0:T(4,128)}, u32[]{:S(2)}) copy-start(f32[5,1024,4]{1,2,0:T(4,128)} %param.34) | copy-start | bytes 245764
  23.0 13.0 %copy-start.33 = (f32[5,4,1024]{2,1,0:T(4,128)S(1)}, f32[5,4,1024]{2,1,0:T(4,128)}, u32[]{:S(2)}) copy-start(f32[5,4,1024]{2,1,0:T(4,128)} %refs_2_.1) | copy-start | bytes 245764
  23.0 13.0 %copy-start.38 = (f32[4096,4]{0,1:T(4,128)S(1)}, f32[4096,4]{0,1:T(4,128)}, u32[]{:S(2)}) copy-start(f32[4096,4]{0,1:T(4,128)} %param.35) | copy-start | bytes 196612
  23.0 13.0 %copy-start.40 = (f32[4,4096]{1,0:T(4,128)S(1)}, f32[4,4096]{1,0:T(4,128)}, u32[]{:S(2)}) copy-start(f32[4,4096]{1,0:T(4,128)} %refs_3_.1) | copy-start | bytes 196612
  35.9 10.7 %collective-permute-start.7 = (bf16[256,1024]{1,0:T(8,128)(2,1)S(1)}, bf16[256,1024]{1,0:T(8,128)(2,1)S(1)}, u32[]{:S(2)}, u32[]{:S(2)}) collective-permute-start(bf16[256,1024]{1,0:T(8,128)(2,1)S(1)} %get-tuple-element.164.hm_ref), channel_id=1, source_target_pairs={{0,1},{1,0},{2,3},{3,2},{4,5},{5,4},{6,7},{7,6},{8,9},{9,8},{10,11... | collective-permute-start | bytes 1572872 | tf_op jit(solution)/shard_map/ppermute | solution.py:842
  52.2 2.3 collective-permute-start.9
  52.3 4.2 %collective-permute-start.8 = (bf16[256,1024]{1,0:T(8,128)(2,1)S(1)}, bf16[256,1024]{1,0:T(8,128)(2,1)S(1)}, u32[]{:S(2)}, u32[]{:S(2)}) collective-permute-start(bf16[256,1024]{1,0:T(8,128)(2,1)S(1)} %get-tuple-element.168.hm_ref), channel_id=1, source_target_pairs={{0,1},{1,0},{2,3},{3,2},{4,5},{5,4},{6,7},{7,6},{8,9},{9,8},{10,11... | collective-permute-start | bytes 1572872 | tf_op jit(solution)/shard_map/ppermute | solution.py:842
  52.8 3.7 %collective-permute-start.1 = (s32[4]{0:T(128)S(1)}, s32[4]{0:T(128)S(1)}, u32[]{:S(2)}, u32[]{:S(2)}) collective-permute-start(s32[4]{0:T(128)S(1)} %fusion.1), channel_id=1, source_target_pairs={{0,8},{4,12},{8,0},{12,4},{16,24},{20,28},{24,16},{28,20},{1,9},{5... | collective-permute-start | bytes 56 | tf_op jit(solution)/shard_map/ppermute | solution.py:842
  54.7 13.7 %collective-permute-start.12 = (bf16[256,1024]{1,0:T(8,128)(2,1)S(1)}, bf16[256,1024]{1,0:T(8,128)(2,1)S(1)}, u32[]{:S(2)}, u32[]{:S(2)}) collective-permute-start(bf16[256,1024]{1,0:T(8,128)(2,1)S(1)} %add_convert_fusion.7.sum_ref), channel_id=1, source_target_pairs={{0,2},{1,3},{2,0},{3,1},{4,6},{5,7},{6,4},{7,5},{8,10},{9,11},{10,... | collective-permute-start | bytes 1572872 | tf_op jit(solution)/shard_map/ppermute | solution.py:842
  65.7 4.3 %collective-permute-start.10 = (bf16[256,1024]{1,0:T(8,128)(2,1)S(1)}, bf16[256,1024]{1,0:T(8,128)(2,1)S(1)}, u32[]{:S(2)}, u32[]{:S(2)}) collective-permute-start(bf16[256,1024]{1,0:T(8,128)(2,1)S(1)} %get-tuple-element.174), channel_id=1, source_target_pairs={{0,1},{1,0},{2,3},{3,2},{4,5},{5,4},{6,7},{7,6},{8,9},{9,8},{10,11... | collective-permute-start | bytes 1572872 | tf_op jit(solution)/shard_map/ppermute | solution.py:842
  69.9 2.0 collective-permute-start.13
  70.1 14.4 %collective-permute-start.11 = (bf16[256,1024]{1,0:T(8,128)(2,1)S(1)}, bf16[256,1024]{1,0:T(8,128)(2,1)S(1)}, u32[]{:S(2)}, u32[]{:S(2)}) collective-permute-start(bf16[256,1024]{1,0:T(8,128)(2,1)S(1)} %add_convert_fusion.6.sum_ref), channel_id=1, source_target_pairs={{0,2},{1,3},{2,0},{3,1},{4,6},{5,7},{6,4},{7,5},{8,10},{9,11},{10,... | collective-permute-start | bytes 1572872 | tf_op jit(solution)/shard_map/ppermute | solution.py:842
  77.7 10.2 %collective-permute-start.14 = (bf16[256,1024]{1,0:T(8,128)(2,1)S(1)}, bf16[256,1024]{1,0:T(8,128)(2,1)S(1)}, u32[]{:S(2)}, u32[]{:S(2)}) collective-permute-start(bf16[256,1024]{1,0:T(8,128)(2,1)S(1)} %get-tuple-element.184), channel_id=1, source_target_pairs={{0,1},{1,0},{2,3},{3,2},{4,5},{5,4},{6,7},{7,6},{8,9},{9,8},{10,11... | collective-permute-start | bytes 1572872 | tf_op jit(solution)/shard_map/ppermute | solution.py:842
  85.0 12.6 %copy-start.20 = (bf16[256,1024]{1,0:T(8,128)(2,1)}, bf16[256,1024]{1,0:T(8,128)(2,1)S(1)}, u32[]{:S(2)}) copy-start(bf16[256,1024]{1,0:T(8,128)(2,1)S(1)} %get-tuple-element.186.hm_ref) | copy-start | bytes 1572868
  85.0 6.3 %collective-permute-start.15 = (bf16[256,1024]{1,0:T(8,128)(2,1)S(1)}, bf16[256,1024]{1,0:T(8,128)(2,1)S(1)}, u32[]{:S(2)}, u32[]{:S(2)}) collective-permute-start(bf16[256,1024]{1,0:T(8,128)(2,1)S(1)} %get-tuple-element.186.hm_ref), channel_id=1, source_target_pairs={{0,1},{1,0},{2,3},{3,2},{4,5},{5,4},{6,7},{7,6},{8,9},{9,8},{10,11... | collective-permute-start | bytes 1572872 | tf_op jit(solution)/shard_map/ppermute | solution.py:842
  85.1 5.7 %collective-permute-start.2 = (s32[4]{0:T(128)S(1)}, s32[4]{0:T(128)S(1)}, u32[]{:S(2)}, u32[]{:S(2)}) collective-permute-start(s32[4]{0:T(128)S(1)} %fusion.5), channel_id=1, source_target_pairs={{0,16},{4,20},{8,24},{12,28},{16,0},{20,4},{24,8},{28,12},{1,17},{... | collective-permute-start | bytes 56 | tf_op jit(solution)/shard_map/ppermute | solution.py:842
  88.9 14.4 %collective-permute-start.17 = (bf16[256,1024]{1,0:T(8,128)(2,1)}, bf16[256,1024]{1,0:T(8,128)(2,1)}, u32[]{:S(2)}, u32[]{:S(2)}) collective-permute-start(bf16[256,1024]{1,0:T(8,128)(2,1)} %add_convert_fusion.5.sum_ref), channel_id=1, source_target_pairs={{0,2},{1,3},{2,0},{3,1},{4,6},{5,7},{6,4},{7,5},{8,10},{9,11},{10,... | collective-permute-start | bytes 1572872 | tf_op jit(solution)/shard_map/ppermute | solution.py:842
  102.3 4.8 %collective-permute-start.16 = (bf16[256,1024]{1,0:T(8,128)(2,1)}, bf16[256,1024]{1,0:T(8,128)(2,1)}, u32[]{:S(2)}, u32[]{:S(2)}) collective-permute-start(bf16[256,1024]{1,0:T(8,128)(2,1)} %get-tuple-element.188), channel_id=1, source_target_pairs={{0,1},{1,0},{2,3},{3,2},{4,5},{5,4},{6,7},{7,6},{8,9},{9,8},{10,11... | collective-permute-start | bytes 1572872 | tf_op jit(solution)/shard_map/ppermute | solution.py:842
  106.3 3.7 %collective-permute-start.18 = (bf16[256,1024]{1,0:T(8,128)(2,1)}, bf16[256,1024]{1,0:T(8,128)(2,1)S(1)}, u32[]{:S(2)}, u32[]{:S(2)}) collective-permute-start(bf16[256,1024]{1,0:T(8,128)(2,1)} %copy-done.71), channel_id=1, source_target_pairs={{0,1},{1,0},{2,3},{3,2},{4,5},{5,4},{6,7},{7,6},{8,9},{9,8},{10,11... | collective-permute-start | bytes 1572872 | tf_op jit(solution)/shard_map/ppermute | solution.py:842
  106.6 5.9 %collective-permute-start.20 = (bf16[256,1024]{1,0:T(8,128)(2,1)S(1)}, bf16[256,1024]{1,0:T(8,128)(2,1)S(1)}, u32[]{:S(2)}, u32[]{:S(2)}) collective-permute-start(bf16[256,1024]{1,0:T(8,128)(2,1)S(1)} %get-tuple-element.200.hm_ref.h_ref), channel_id=1, source_target_pairs={{0,1},{1,0},{2,3},{3,2},{4,5},{5,4},{6,7},{7,6},{8,9},{9,8},{10,11... | collective-permute-start | bytes 1572872 | tf_op jit(solution)/shard_map/ppermute | solution.py:842
  106.9 3.8 %collective-permute-start.19 = (bf16[256,1024]{1,0:T(8,128)(2,1)S(1)}, bf16[256,1024]{1,0:T(8,128)(2,1)S(1)}, u32[]{:S(2)}, u32[]{:S(2)}) collective-permute-start(bf16[256,1024]{1,0:T(8,128)(2,1)S(1)} %copy-done.70), channel_id=1, source_target_pairs={{0,1},{1,0},{2,3},{3,2},{4,5},{5,4},{6,7},{7,6},{8,9},{9,8},{10,11... | collective-permute-start | bytes 1572872 | tf_op jit(solution)/shard_map/ppermute | solution.py:842
  108.3 48.4 %collective-permute-start.23 = (bf16[256,1024]{1,0:T(8,128)(2,1)S(1)}, bf16[256,1024]{1,0:T(8,128)(2,1)S(1)}, u32[]{:S(2)}, u32[]{:S(2)}) collective-permute-start(bf16[256,1024]{1,0:T(8,128)(2,1)S(1)} %add_convert_fusion.4.sum_ref), channel_id=1, source_target_pairs={{0,2},{1,3},{2,0},{3,1},{4,6},{5,7},{6,4},{7,5},{8,10},{9,11},{10,... | collective-permute-start | bytes 1572872 | tf_op jit(solution)/shard_map/ppermute | solution.py:842
  110.2 46.4 %collective-permute-start.21 = (bf16[256,1024]{1,0:T(8,128)(2,1)S(1)}, bf16[256,1024]{1,0:T(8,128)(2,1)S(1)}, u32[]{:S(2)}, u32[]{:S(2)}) collective-permute-start(bf16[256,1024]{1,0:T(8,128)(2,1)S(1)} %add_convert_fusion.3.row_ref), channel_id=1, source_target_pairs={{0,2},{1,3},{2,0},{3,1},{4,6},{5,7},{6,4},{7,5},{8,10},{9,11},{10,... | collective-permute-start | bytes 1572872 | tf_op jit(solution)/shard_map/ppermute | solution.py:842
  110.9 45.8 %collective-permute-start.22 = (bf16[256,1024]{1,0:T(8,128)(2,1)S(1)}, bf16[256,1024]{1,0:T(8,128)(2,1)S(1)}, u32[]{:S(2)}, u32[]{:S(2)}) collective-permute-start(bf16[256,1024]{1,0:T(8,128)(2,1)S(1)} %add_convert_fusion.2.row_ref), channel_id=1, source_target_pairs={{0,2},{1,3},{2,0},{3,1},{4,6},{5,7},{6,4},{7,5},{8,10},{9,11},{10,... | collective-permute-start | bytes 1572872 | tf_op jit(solution)/shard_map/ppermute | solution.py:842
  156.6 2.0 collective-permute-start.24
  157.2 2.4 collective-permute-start.25
  159.2 35.1 %collective-permute-start.28 = (bf16[272,1024]{1,0:T(8,128)(2,1)S(1)}, bf16[272,1024]{1,0:T(8,128)(2,1)S(1)}, u32[]{:S(2)}, u32[]{:S(2)}) collective-permute-start(bf16[272,1024]{1,0:T(8,128)(2,1)S(1)} %get-tuple-element.208.total_ref), channel_id=1, source_target_pairs={{0,2},{1,3},{2,0},{3,1},{4,6},{5,7},{6,4},{7,5},{8,10},{9,11},{10,... | collective-permute-start | bytes 1671176 | tf_op jit(solution)/shard_map/ppermute | solution.py:842
  159.6 38.7 %copy-start.29 = (bf16[256,1024]{1,0:T(8,128)(2,1)S(1)}, bf16[256,1024]{1,0:T(8,128)(2,1)}, u32[]{:S(2)}) copy-start(bf16[256,1024]{1,0:T(8,128)(2,1)} %copy-done.28) | copy-start | bytes 1572868
  159.6 38.7 %copy-start.31 = (bf16[256,1024]{1,0:T(8,128)(2,1)S(1)}, bf16[256,1024]{1,0:T(8,128)(2,1)}, u32[]{:S(2)}) copy-start(bf16[256,1024]{1,0:T(8,128)(2,1)} %copy-done.30) | copy-start | bytes 1572868
  159.6 38.7 %copy-start.49 = (bf16[2,256,16]{2,1,0:T(8,128)(2,1)S(1)}, bf16[2,256,16]{2,1,0:T(8,128)(2,1)}, u32[]{:S(2)}) copy-start(bf16[2,256,16]{2,1,0:T(8,128)(2,1)} %copy-done.48) | copy-start | bytes 49156
  194.1 2.1 collective-permute-start.26
  195.6 2.7 collective-permute-start.29
  196.7 14.7 %collective-permute-start.27 = (bf16[272,1024]{1,0:T(8,128)(2,1)S(1)}, bf16[272,1024]{1,0:T(8,128)(2,1)S(1)}, u32[]{:S(2)}, u32[]{:S(2)}) collective-permute-start(bf16[272,1024]{1,0:T(8,128)(2,1)S(1)} %get-tuple-element.213.total_ref), channel_id=1, source_target_pairs={{0,2},{1,3},{2,0},{3,1},{4,6},{5,7},{6,4},{7,5},{8,10},{9,11},{10,... | collective-permute-start | bytes 1671176 | tf_op jit(solution)/shard_map/ppermute | solution.py:842
  204.6 8.2 %collective-permute-start.30 = (bf16[256,1024]{1,0:T(8,128)(2,1)S(1)}, bf16[256,1024]{1,0:T(8,128)(2,1)S(1)}, u32[]{:S(2)}, u32[]{:S(2)}) collective-permute-start(bf16[256,1024]{1,0:T(8,128)(2,1)S(1)} %get-tuple-element.227), channel_id=1, source_target_pairs={{0,1},{1,0},{2,3},{3,2},{4,5},{5,4},{6,7},{7,6},{8,9},{9,8},{10,11... | collective-permute-start | bytes 1572872 | tf_op jit(solution)/shard_map/ppermute | solution.py:842
  212.8 2.0 collective-permute-start.31
  213.0 14.4 %collective-permute-start.32 = (bf16[256,1024]{1,0:T(8,128)(2,1)S(1)}, bf16[256,1024]{1,0:T(8,128)(2,1)S(1)}, u32[]{:S(2)}, u32[]{:S(2)}) collective-permute-start(bf16[256,1024]{1,0:T(8,128)(2,1)S(1)} %add_convert_fusion.1.sum_ref), channel_id=1, source_target_pairs={{0,2},{1,3},{2,0},{3,1},{4,6},{5,7},{6,4},{7,5},{8,10},{9,11},{10,... | collective-permute-start | bytes 1572872 | tf_op jit(solution)/shard_map/ppermute | solution.py:842
  214.8 12.6 %copy-start.5 = (f32[256,1024]{1,0:T(8,128)S(1)}, f32[256,1024]{1,0:T(8,128)}, u32[]{:S(2)}) copy-start(f32[256,1024]{1,0:T(8,128)} %copy-done.3) | copy-start | bytes 3145732
  221.2 8.1 %collective-permute-start.33 = (bf16[256,1024]{1,0:T(8,128)(2,1)S(1)}, bf16[256,1024]{1,0:T(8,128)(2,1)S(1)}, u32[]{:S(2)}, u32[]{:S(2)}) collective-permute-start(bf16[256,1024]{1,0:T(8,128)(2,1)S(1)} %get-tuple-element.238), channel_id=1, source_target_pairs={{0,1},{1,0},{2,3},{3,2},{4,5},{5,4},{6,7},{7,6},{8,9},{9,8},{10,11... | collective-permute-start | bytes 1572872 | tf_op jit(solution)/shard_map/ppermute | solution.py:842
  229.2 2.0 collective-permute-start.34
  229.4 14.4 %collective-permute-start.35 = (bf16[256,1024]{1,0:T(8,128)(2,1)S(1)}, bf16[256,1024]{1,0:T(8,128)(2,1)S(1)}, u32[]{:S(2)}, u32[]{:S(2)}) collective-permute-start(bf16[256,1024]{1,0:T(8,128)(2,1)S(1)} %add_convert_fusion.sum_ref), channel_id=1, source_target_pairs={{0,2},{1,3},{2,0},{3,1},{4,6},{5,7},{6,4},{7,5},{8,10},{9,11},{10,... | collective-permute-start | bytes 1572872 | tf_op jit(solution)/shard_map/ppermute | solution.py:842
  245.6 1.9 collective-permute-start.36
  259.0 25.7 %copy-start.39 = (f32[4096,4]{0,1:T(4,128)S(1)}, f32[4096,4]{0,1:T(4,128)}, u32[]{:S(2)}) copy-start(f32[4096,4]{0,1:T(4,128)} %param.35) | copy-start | bytes 196612
  259.1 25.7 %copy-start.41 = (f32[4,4096]{1,0:T(4,128)S(1)}, f32[4,4096]{1,0:T(4,128)}, u32[]{:S(2)}) copy-start(f32[4,4096]{1,0:T(4,128)} %refs_3_.1) | copy-start | bytes 196612
  259.1 25.7 %copy-start.58 = (f32[5,1024,4]{1,2,0:T(4,128)S(1)}, f32[5,1024,4]{1,2,0:T(4,128)}, u32[]{:S(2)}) copy-start(f32[5,1024,4]{1,2,0:T(4,128)} %param.38) | copy-start | bytes 245764
  259.1 25.7 %copy-start.59 = (f32[5,4,1024]{2,1,0:T(4,128)S(1)}, f32[5,4,1024]{2,1,0:T(4,128)}, u32[]{:S(2)}) copy-start(f32[5,4,1024]{2,1,0:T(4,128)} %refs_6_.1) | copy-start | bytes 245764
  259.1 25.7 %copy-start.60 = (f32[5,1024,4]{1,2,0:T(4,128)S(1)}, f32[5,1024,4]{1,2,0:T(4,128)}, u32[]{:S(2)}) copy-start(f32[5,1024,4]{1,2,0:T(4,128)} %param.42) | copy-start | bytes 245764
  259.1 25.7 %copy-start.61 = (f32[5,4,1024]{2,1,0:T(4,128)S(1)}, f32[5,4,1024]{2,1,0:T(4,128)}, u32[]{:S(2)}) copy-start(f32[5,4,1024]{2,1,0:T(4,128)} %refs_10_.1) | copy-start | bytes 245764
  259.1 25.7 %copy-start.62 = (f32[4096,4]{0,1:T(4,128)S(1)}, f32[4096,4]{0,1:T(4,128)}, u32[]{:S(2)}) copy-start(f32[4096,4]{0,1:T(4,128)} %param.39) | copy-start | bytes 196612
  259.1 25.7 %copy-start.63 = (f32[4,4096]{1,0:T(4,128)S(1)}, f32[4,4096]{1,0:T(4,128)}, u32[]{:S(2)}) copy-start(f32[4,4096]{1,0:T(4,128)} %refs_7_.1) | copy-start | bytes 196612
  259.1 25.7 %copy-start.64 = (f32[4096,4]{0,1:T(4,128)S(1)}, f32[4096,4]{0,1:T(4,128)}, u32[]{:S(2)}) copy-start(f32[4096,4]{0,1:T(4,128)} %param.43) | copy-start | bytes 196612
  259.2 25.7 %copy-start.65 = (f32[4,4096]{1,0:T(4,128)S(1)}, f32[4,4096]{1,0:T(4,128)}, u32[]{:S(2)}) copy-start(f32[4,4096]{1,0:T(4,128)} %refs_11_.1) | copy-start | bytes 196612
  259.2 1.3 collective-permute-start.37
  260.6 3.9 %collective-permute-start.38 = (f32[4,1536]{1,0:T(4,128)S(1)}, f32[4,1536]{1,0:T(4,128)S(1)}, u32[]{:S(2)}, u32[]{:S(2)}) collective-permute-start(f32[4,1536]{1,0:T(4,128)S(1)} %constant_dynamic-slice_fusion), channel_id=1, source_target_pairs={{0,2},{1,3},{2,0},{3,1},{4,6},{5,7},{6,4},{7,5},{8,10},{9,11},{10,... | collective-permute-start | bytes 73736 | tf_op jit(solution)/shard_map/ppermute | solution.py:842
  264.5 4.4 %collective-permute-start.39 = (f32[4,4736]{1,0:T(4,128)S(1)}, f32[4,4736]{1,0:T(4,128)S(1)}, u32[]{:S(2)}, u32[]{:S(2)}) collective-permute-start(f32[4,4736]{1,0:T(4,128)S(1)} %pad_maximum_fusion), channel_id=1, source_target_pairs={{0,4},{4,0},{8,12},{12,8},{16,20},{20,16},{24,28},{28,24},{1,5},{5... | collective-permute-start | bytes 227336 | tf_op jit(solution)/shard_map/ppermute | solution.py:842
  269.0 4.4 %collective-permute-start.40 = (f32[4,4736]{1,0:T(4,128)S(1)}, f32[4,4736]{1,0:T(4,128)S(1)}, u32[]{:S(2)}, u32[]{:S(2)}) collective-permute-start(f32[4,4736]{1,0:T(4,128)S(1)} %fusion.2), channel_id=1, source_target_pairs={{0,8},{4,12},{8,0},{12,4},{16,24},{20,28},{24,16},{28,20},{1,9},{5... | collective-permute-start | bytes 227336 | tf_op jit(solution)/shard_map/ppermute | solution.py:842
  273.4 5.3 %collective-permute-start.41 = (f32[4,4736]{1,0:T(4,128)S(1)}, f32[4,4736]{1,0:T(4,128)S(1)}, u32[]{:S(2)}, u32[]{:S(2)}) collective-permute-start(f32[4,4736]{1,0:T(4,128)S(1)} %add.100), channel_id=1, source_target_pairs={{0,16},{4,20},{8,24},{12,28},{16,0},{20,4},{24,8},{28,12},{1,17},{... | collective-permute-start | bytes 227336 | tf_op jit(solution)/shard_map/ppermute | solution.py:842
  278.8 4.4 %collective-permute-start.42 = (f32[1,4,4736]{2,1,0:T(4,128)S(1)}, f32[1,4,4736]{2,1,0:T(4,128)S(1)}, u32[]{:S(2)}, u32[]{:S(2)}) collective-permute-start(f32[1,4,4736]{2,1,0:T(4,128)S(1)} %add_bitcast_fusion), channel_id=1, source_target_pairs={{0,2},{1,3},{2,0},{3,1},{4,6},{5,7},{6,4},{7,5},{8,10},{9,11},{10,... | collective-permute-start | bytes 227336 | tf_op jit(solution)/shard_map/ppermute | solution.py:842
  283.3 1.4 collective-permute-start.43
  (71 other events, 334.0 us)
where the time goes:
time: 291 us; the launch traced here: 287 us
  Pallas kernels  171 us (59%)
  waiting for transfers between devices  56.1 us (19%)
  starting transfers between devices  36 us (12%)
  local copies, waits for them, and re-layouts  14.7 us (5%)
  other arithmetic  5.48 us (2%)
  between operations  3.5 us (1%)
    pallas_call x2, Pallas kernels, head(): pl.pallas_call(functools.partial(head_kernel, block), out_shape=(shape((h...  78.5 us
    pallas_call x27, Pallas kernels, call(): pl.pallas_call(kernel, out_shape=tuple(outs), in_specs=specs, out_specs=t...  70 us
    ppermute x44, waiting for transfers between devices, swap(): return lax.ppermute(value, axis, [(i, i ^ step) for i in range(size)])  56.1 us
    ppermute x44, starting transfers between devices, swap(): return lax.ppermute(value, axis, [(i, i ^ step) for i in range(size)])  36 us
    pallas_call x2, Pallas kernels, gather(): pl.pallas_call(gather_kernel, out_shape=tuple((shape((half, width), bf16)...  22.5 us
    unnamed x182, local copies, waits for them, and re-layouts  12.4 us
  transfers between devices with their start and end apart: 44, of which 19 were waited for; matrix products, arithmetic and copies ran while one was open for 2% of the time, Pallas kernels for 49%

commit v1 on v0

--- a/solution.py
+++ b/solution.py
@@ -73,7 +73,7 @@
     return jnp.where((column >= width) & (column < 2 * width), low, high)
 
 
-def gather_kernel(place_ref, ids_ref, table, *refs):
+def gather_kernel(first, place_ref, ids_ref, table, *refs):
     outs = refs[:-3]
     buf, sems, counts = refs[-3:]
     side = place_ref[0]
@@ -82,7 +82,7 @@
     vocab = table.shape[0]
 
     def base(g):
-        return (g // 2 * 2 + (side if g % 2 == 0 else 1 - side)) * half
+        return (2 * first + g // 2 * 2 + (side if g % 2 == 0 else 1 - side)) * half
 
     def find(position):
         local = ids_ref[position] - offset
@@ -133,11 +133,11 @@
         lax.fori_loop(0, half // 16, extract, 0)
 
 
-def gather(place, ids, table, half):
-    count = ids.shape[0] // half
+def gather(place, ids, table, half, first, count):
+    count = 2 * count
     width = table.shape[1]
     return pl.pallas_call(
-        gather_kernel,
+        functools.partial(gather_kernel, first),
         out_shape=tuple(shape((half, width), bf16) for _ in range(count)),
         in_specs=[SM, SM, HBM],
         out_specs=(VM,) * count,
@@ -855,10 +855,6 @@
 
     gather_place = jnp.stack([side, index * vocab]).astype(jnp.int32)
 
-    def lookup(ids):
-        rows = gather(gather_place, ids.reshape(-1), embedding, half)
-        return [rows[2 * n : 2 * n + 2] for n in range(CHUNKS)]
-
     down = jnp.swapaxes(model_down_maps, 1, 2)
     hidden_down = jnp.swapaxes(hidden_down_map, 0, 1)
     (
@@ -885,17 +881,27 @@
         counts.append(counts[-1] + swap(counts[-1], step, "batch"))
         return after(value, counts[-1])
 
-    embedded = [reduce_rows(*rows) for rows in lookup(token_ids)]
-    wanted_rows = lookup(after(targets, *(pair[0] for pair in embedded)))
+    embedded = []
+    place = gather_place
+    for n in range(CHUNKS):
+        mine, theirs = gather(place, token_ids.reshape(-1), embedding, half, n, 1)
+        if n:
+            mine = after(mine, embedded[0][1])
+        embedded.append(reduce_rows(mine, theirs))
+        place = after(gather_place, embedded[-1][0])
+    wanted = after(targets, embedded[0][1], *(pair[0] for pair in embedded))
+    rows = gather(gather_place, wanted.reshape(-1), embedding, half, 0, CHUNKS)
+    wanted_rows = [rows[2 * n : 2 * n + 2] for n in range(CHUNKS)]
     held = lax.optimization_barrier(
         (count_step(embedded[0][0]), *(row for pair in wanted_rows for row in pair))
     )
     embedded[0] = (held[0], embedded[0][1])
     wanted_rows = [held[1 + 2 * n : 3 + 2 * n] for n in range(CHUNKS)]
     x0, qkv, h1, u1, normed = [], [], [], [], []
+    ready = after(side, embedded[0][1])
     for n in range(CHUNKS):
         x, h = norm_forward(
-            0, *embedded[n], pick(position_halves[n], side), norm_gains, norm_shifts
+            0, *embedded[n], pick(position_halves[n], ready), norm_gains, norm_shifts
         )
         x0.append(x)
         normed.append((h, swap(h, 1)))

time: 291 us -> 310 us (1.065)
  Pallas kernels: 171 us -> 185 us
  local copies, waits for them, and re-layouts: 14.7 us -> 28.2 us
  starting transfers between devices: 36 us -> 31.7 us
  waiting for transfers between devices: 56.1 us -> 52.2 us
    pallas_call x2 -> x3, Pallas kernels: 22.5 us -> 37.3 us  [gather(): pl.pallas_call(functools.partial(gather_kernel, first), out_shape=tuple((...]
    unnamed x182 -> x184, local copies, waits for them, and re-layouts: 12.4 us -> 24 us
    ppermute x44, starting transfers between devices: 36 us -> 31.7 us  [swap(): return lax.ppermute(value, axis, [(i, i ^ step) for i in range(size)])]
    ppermute x44, waiting for transfers between devices: 56.1 us -> 52.2 us  [swap(): return lax.ppermute(value, axis, [(i, i ^ step) for i in range(size)])]
  transfers between devices with their start and end apart: 44 -> 44, of which waited for: 19 -> 20; matrix products, arithmetic and copies ran while one was open for 2% -> 3% of each run, Pallas kernels for 49% -> 50%
where the time goes in v1:
time: 310 us; the launch traced here: 305 us
  Pallas kernels  185 us (60%)
  waiting for transfers between devices  52.2 us (17%)
  starting transfers between devices  31.7 us (10%)
  local copies, waits for them, and re-layouts  28.2 us (9%)
  other arithmetic  4.47 us (1%)
  between operations  3.49 us (1%)
    pallas_call x2, Pallas kernels, head(): pl.pallas_call(functools.partial(head_kernel, block), out_shape=(shape((h...  78.5 us
    pallas_call x27, Pallas kernels, call(): pl.pallas_call(kernel, out_shape=tuple(outs), in_specs=specs, out_specs=t...  69.7 us
    ppermute x44, waiting for transfers between devices, swap(): return lax.ppermute(value, axis, [(i, i ^ step) for i in range(size)])  52.2 us
    pallas_call x3, Pallas kernels, gather(): pl.pallas_call(functools.partial(gather_kernel, first), out_shape=tuple((...  37.3 us
    ppermute x44, starting transfers between devices, swap(): return lax.ppermute(value, axis, [(i, i ^ step) for i in range(size)])  31.7 us
    unnamed x184, local copies, waits for them, and re-layouts  24 us
  transfers between devices with their start and end apart: 44, of which 20 were waited for; matrix products, arithmetic and copies ran while one was open for 3% of the time, Pallas kernels for 50%

profile of v1, /device:TPU:0, one launch (start us, length us, event | category | flops | bytes accessed | tf_op | source)
XLA Modules:
  0.0 305.5 jit_solution(12860772458337905274)
XLA Ops:
  0.7 8.3 %copy-done = bf16[12576,1024]{1,0:T(8,128)(2,1)S(1)} copy-done((bf16[12576,1024]{1,0:T(8,128)(2,1)S(1)}, bf16[12576,1024]{1,0:T(8,128)(2,1)}, u32[]{:S(2)}) %copy-start) | copy-done | bytes 25755672
  9.7 12.5 %gather.3 = (bf16[256,1024]{1,0:T(8,128)(2,1)S(1)}, bf16[256,1024]{1,0:T(8,128)(2,1)S(1)}) custom-call(s32[2]{0:T(128)S(1)} %pad_add_fusion.place_ref, s32[1024]{0:T(1024)S(1)} %bitcast.42, bf16[12576,1024]{1,0:T(8,128)(2,1)S(1)} %copy-done), custom_call_target="tpu_custom_call" | custom-call | flops 1 | bytes 8388608 | tf_op jit(solution)/shard_map/gather/pallas_call | solution.py:139
  23.6 2.5 collective-permute-start
  26.3 1.0 collective-permute-start.4
  27.3 12.7 %gather.4 = (bf16[256,1024]{1,0:T(8,128)(2,1)S(1)}, bf16[256,1024]{1,0:T(8,128)(2,1)S(1)}) custom-call(s32[2]{0:T(128)S(1)} %pad_add_fusion.place_ref, s32[1024]{0:T(1024)S(1)} %bitcast.43, bf16[12576,1024]{1,0:T(8,128)(2,1)S(1)} %copy-done), custom_call_target="tpu_custom_call" | custom-call | flops 1 | bytes 8388608 | tf_op jit(solution)/shard_map/gather/pallas_call | solution.py:139
  40.1 1.5 fusion.3
  42.8 12.1 %gather.5 = (bf16[256,1024]{1,0:T(8,128)(2,1)S(1)}, bf16[256,1024]{1,0:T(8,128)(2,1)S(1)}, bf16[256,1024]{1,0:T(8,128)(2,1)S(1)}, bf16[256,1024]{1,0:T(8,128)(2,1)S(1)}) custom-call(s32[2]{0:T(128)S(1)} %pad_add_fusion.place_ref, s32[1024]{0:T(1024)S(1)} %bitcast.44, bf16[12576,1024]{1,0:T(8,128)(2,1)} %table.9), custom_call_target="tpu_custom_call" | custom-call | flops 1 | bytes 16777216 | tf_op jit(solution)/shard_map/gather/pallas_call | solution.py:139
  58.1 1.1 dynamic-slice_bitcast_fusion.1.x_ref
  63.5 1.1 dynamic-slice_bitcast_fusion.x_ref
  65.1 1.8 qkv.2
  67.0 3.8 %attention_0.1 = (f32[256,1024]{1,0:T(8,128)S(1)}, bf16[256,1024]{1,0:T(8,128)(2,1)S(1)}, bf16[2,256,256]{2,1,0:T(8,128)(2,1)S(1)}, f32[8,512]{1,0:T(8,128)S(1)}, bf16[2,256,16]{2,1,0:T(8,128)(2,1)S(1)}) custom-call(s32[1]{0:T(128)} %bitcast.side_ref, bf16[256,1024]{1,0:T(8,128)(2,1)S(1)} %copy-done.11, bf16[16,256]{1,0:T(8,128)(2,1)S(1)} %get-tuple-element.152.a_ref, ...), custom_call_target="tpu_custom_call" | custom-call | flops 671088640 | bytes 3219460 | tf_op jit(solution)/shard_map/attention_0/pallas_call | solution.py:51
  71.4 1.6 collective-permute-start.1
  73.9 1.1 collective-permute-done.1
  75.0 1.8 qkv.3
  76.8 1.0 copy-done.77
  77.8 6.3 %attention_1.1 = (f32[256,1024]{1,0:T(8,128)S(1)}, bf16[256,1024]{1,0:T(8,128)(2,1)S(1)}, bf16[2,256,256]{2,1,0:T(8,128)(2,1)S(1)}, f32[8,512]{1,0:T(8,128)S(1)}, bf16[2,256,16]{2,1,0:T(8,128)(2,1)S(1)}) custom-call(s32[1]{0:T(128)} %bitcast.side_ref, bf16[256,1024]{1,0:T(8,128)(2,1)S(1)} %copy-done.11, bf16[16,256]{1,0:T(8,128)(2,1)S(1)} %get-tuple-element.152.a_ref, ...), custom_call_target="tpu_custom_call" | custom-call | flops 1207959552 | bytes 4005892 | tf_op jit(solution)/shard_map/attention_1/pallas_call | solution.py:51
  84.2 3.2 %collective-permute-done.12.got_ref = bf16[256,1024]{1,0:T(8,128)(2,1)S(1)} collective-permute-done((bf16[256,1024]{1,0:T(8,128)(2,1)S(1)}, bf16[256,1024]{1,0:T(8,128)(2,1)S(1)}, u32[]{:S(2)}, u32[]{:S(2)}) %collective-permute-start.12) | collective-permute-done | bytes 524320 | tf_op jit(solution)/shard_map/ppermute | solution.py:842
  87.8 1.0 copy-done.4
  90.7 5.7 %mlp.2 = (f32[256,1024]{1,0:T(8,128)S(1)}, bf16[256,1024]{1,0:T(8,128)(2,1)S(1)}, bf16[2,256,1024]{2,1,0:T(8,128)(2,1)S(1)}, f32[2,256,1024]{2,1,0:T(8,128)S(1)}...) custom-call(bf16[256,1024]{1,0:T(8,128)(2,1)S(1)} %get-tuple-element.184.hm_ref, ...), custom_call_target="tpu_custom_call" | custom-call | flops 2147483648 | bytes 10125312 | tf_op jit(solution)/shard_map/mlp/pallas_call | solution.py:51
  96.7 6.7 %collective-permute-done.11.got_ref = bf16[256,1024]{1,0:T(8,128)(2,1)S(1)} collective-permute-done((bf16[256,1024]{1,0:T(8,128)(2,1)S(1)}, bf16[256,1024]{1,0:T(8,128)(2,1)S(1)}, u32[]{:S(2)}, u32[]{:S(2)}) %collective-permute-start.11) | collective-permute-done | bytes 524320 | tf_op jit(solution)/shard_map/ppermute | solution.py:842
  103.9 2.9 collective-permute-start.2
  106.8 0.9 add_convert_fusion.5.sum_ref
  107.8 1.3 collective-permute-start.17
  109.7 6.2 %mlp.3 = (f32[256,1024]{1,0:T(8,128)S(1)}, bf16[256,1024]{1,0:T(8,128)(2,1)}, bf16[2,256,1024]{2,1,0:T(8,128)(2,1)S(1)}, f32[2,256,1024]{2,1,0:T(8,128)S(1)}, bf...) custom-call(bf16[256,1024]{1,0:T(8,128)(2,1)S(1)} %get-tuple-element.192.hm_ref, ...), custom_call_target="tpu_custom_call" | custom-call | flops 2147483648 | bytes 10125312 | tf_op jit(solution)/shard_map/mlp/pallas_call | solution.py:51
  115.9 1.4 copy-done.7
  117.3 1.0 copy-done.14
  118.3 1.0 copy-done.18
  122.1 1.2 copy-done.5
  123.4 1.8 norm_forward_2.2
  125.8 1.2 add_convert_fusion.4.sum_ref
  127.1 1.3 collective-permute-start.23
  129.6 1.3 collective-permute-start.22
  130.9 44.1 %vocabulary_head.2 = (f32[256,1024]{1,0:T(8,128)S(1)}, bf16[272,1024]{1,0:T(8,128)(2,1)S(1)}, f32[8,256]{1,0:T(8,128)S(1)}) custom-call(bf16[256,1024]{1,0:T(8,128)(2,1)S(1)} %get-tuple-element.206.hm_ref.h_ref, bf16[256,1024]{1,0:T(8,128)(2,1)S(1)} %collective-permute-done.20.ho_ref, bf16[12576,1024]{1,0:T(8,128)(2,1)} %table.9), custom_call_target="tpu_custom_call" | custom-call | flops 26373783552 | bytes 25755648 | tf_op jit(solution)/shard_map/vocabulary_head/pallas_call | solution.py:387
  178.4 34.5 %vocabulary_head.3 = (f32[256,1024]{1,0:T(8,128)S(1)}, bf16[272,1024]{1,0:T(8,128)(2,1)S(1)}, f32[8,256]{1,0:T(8,128)S(1)}) custom-call(bf16[256,1024]{1,0:T(8,128)(2,1)S(1)} %get-tuple-element.215.hm_ref.h_ref, bf16[256,1024]{1,0:T(8,128)(2,1)S(1)} %collective-permute-done.25.ho_ref, bf16[12576,1024]{1,0:T(8,128)(2,1)} %table.9), custom_call_target="tpu_custom_call" | custom-call | flops 26373783552 | bytes 25755648 | tf_op jit(solution)/shard_map/vocabulary_head/pallas_call | solution.py:387
  213.0 1.4 loss_backward.3
  215.5 1.3 collective-permute-start.27
  216.8 6.2 %mlp_back.2 = (f32[256,1024]{1,0:T(8,128)S(1)}, bf16[256,1024]{1,0:T(8,128)(2,1)S(1)}, f32[16,4096]{1,0:T(8,128)S(1)}) custom-call(bf16[256,1024]{1,0:T(8,128)(2,1)S(1)} %get-tuple-element.226.dm_ref, bf16[256,1024]{1,0:T(8,128)(2,1)S(1)} %collective-permute-done.29.do_ref, bf16[256,1024]{1,0:T(8,128)(2,1)S(1)} %copy-done.30, ...), custom_call_target="tpu_custom_call" | custom-call | flops 2147483648 | bytes 11501568 | tf_op jit(solution)/shard_map/mlp_back/pallas_call | solution.py:51
  223.2 6.9 %collective-permute-done.27.got_ref = bf16[272,1024]{1,0:T(8,128)(2,1)S(1)} collective-permute-done((bf16[272,1024]{1,0:T(8,128)(2,1)S(1)}, bf16[272,1024]{1,0:T(8,128)(2,1)S(1)}, u32[]{:S(2)}, u32[]{:S(2)}) %collective-permute-start.27) | collective-permute-done | bytes 557088 | tf_op jit(solution)/shard_map/ppermute | solution.py:842
  230.1 1.4 loss_backward.2
  231.8 1.3 collective-permute-start.32
  233.6 6.4 %mlp_back.3 = (f32[256,1024]{1,0:T(8,128)S(1)}, bf16[256,1024]{1,0:T(8,128)(2,1)S(1)}, f32[16,4096]{1,0:T(8,128)S(1)}) custom-call(bf16[256,1024]{1,0:T(8,128)(2,1)S(1)} %get-tuple-element.234.dm_ref, bf16[256,1024]{1,0:T(8,128)(2,1)S(1)} %collective-permute-done.31.do_ref, bf16[256,1024]{1,0:T(8,128)(2,1)S(1)} %copy-done.22, ...), custom_call_target="tpu_custom_call" | custom-call | flops 2147483648 | bytes 11763712 | tf_op jit(solution)/shard_map/mlp_back/pallas_call | solution.py:51
  240.1 6.0 %collective-permute-done.32.got_ref = bf16[256,1024]{1,0:T(8,128)(2,1)S(1)} collective-permute-done((bf16[256,1024]{1,0:T(8,128)(2,1)S(1)}, bf16[256,1024]{1,0:T(8,128)(2,1)S(1)}, u32[]{:S(2)}, u32[]{:S(2)}) %collective-permute-start.32) | collective-permute-done | bytes 524320 | tf_op jit(solution)/shard_map/ppermute | solution.py:842
  246.2 1.7 norm_backward_1.2
  248.2 1.3 collective-permute-start.35
  249.9 2.0 output_back.2
  251.9 5.4 %attention_back_0.1 = (f32[3,48,256]{2,1,0:T(8,128)S(1)}, f32[48,1024]{1,0:T(8,128)S(1)}) custom-call(bf16[6,48,256]{2,1,0:T(8,128)(2,1)S(1)} %copy-done.74, bf16[2,256,256]{2,1,0:T(8,128)(2,1)S(1)} %get-tuple-element.250.grad_in, f32[8,512]{1,0:T(8,128)S(1)} %copy-done.88, bf16[3,2,256,256]{3,2,1,0:T(8,128)(2,1)S(1)} %copy-done.80, ...), custom_call_target="tpu_custom_call" | custom-call | flops 1342177280 | bytes 2654208 | tf_op jit(solution)/shard_map/attention_back_0/pallas_call | solution.py:51
  257.4 5.1 %collective-permute-done.35.got_ref = bf16[256,1024]{1,0:T(8,128)(2,1)S(1)} collective-permute-done((bf16[256,1024]{1,0:T(8,128)(2,1)S(1)}, bf16[256,1024]{1,0:T(8,128)(2,1)S(1)}, u32[]{:S(2)}, u32[]{:S(2)}) %collective-permute-start.35) | collective-permute-done | bytes 524320 | tf_op jit(solution)/shard_map/ppermute | solution.py:842
  262.6 1.7 norm_backward_1.3
  264.3 1.9 collective-permute-done.36.do_ref
  266.2 2.0 output_back.3
  268.2 9.4 %attention_back_1.1 = (f32[3,48,256]{2,1,0:T(8,128)S(1)}, f32[48,1024]{1,0:T(8,128)S(1)}) custom-call(bf16[6,48,256]{2,1,0:T(8,128)(2,1)S(1)} %copy-done.74, bf16[2,256,256]{2,1,0:T(8,128)(2,1)S(1)} %get-tuple-element.261.grad_in, f32[8,512]{1,0:T(8,128)S(1)} %copy-done.90, bf16[3,2,256,256]{3,2,1,0:T(8,128)(2,1)S(1)} %copy-done.80, ...), custom_call_target="tpu_custom_call" | custom-call | flops 2684354560 | bytes 4882432 | tf_op jit(solution)/shard_map/attention_back_1/pallas_call | solution.py:51
  278.0 1.1 collective-permute-done.37
  279.2 1.3 collective-permute-start.38
  280.5 2.6 collective-permute-done.38
  283.1 1.5 collective-permute-start.39
  284.6 2.9 collective-permute-done.39
  287.6 1.7 collective-permute-start.40
  289.3 2.7 collective-permute-done.40
  292.0 1.9 collective-permute-start.41
  293.9 3.5 %collective-permute-done.41 = f32[4,4736]{1,0:T(4,128)S(1)} collective-permute-done((f32[4,4736]{1,0:T(4,128)S(1)}, f32[4,4736]{1,0:T(4,128)S(1)}, u32[]{:S(2)}, u32[]{:S(2)}) %collective-permute-start.41) | collective-permute-done | bytes 75808 | tf_op jit(solution)/shard_map/ppermute | solution.py:842
  297.4 1.3 collective-permute-start.42
  298.7 3.1 %collective-permute-done.42 = f32[1,4,4736]{2,1,0:T(4,128)S(1)} collective-permute-done((f32[1,4,4736]{2,1,0:T(4,128)S(1)}, f32[1,4,4736]{2,1,0:T(4,128)S(1)}, u32[]{:S(2)}, u32[]{:S(2)}) %collective-permute-start.42) | collective-permute-done | bytes 75808 | tf_op jit(solution)/shard_map/ppermute | solution.py:842
  302.0 1.4 collective-permute-done.43
  303.5 1.2 adam.1
  (270 shorter events, 27.6 us)
Async XLA Ops:
  22.2 3.8 %collective-permute-start.3 = (bf16[256,1024]{1,0:T(8,128)(2,1)S(1)}, bf16[256,1024]{1,0:T(8,128)(2,1)S(1)}, u32[]{:S(2)}, u32[]{:S(2)}) collective-permute-start(bf16[256,1024]{1,0:T(8,128)(2,1)S(1)} %get-tuple-element.155), channel_id=1, source_target_pairs={{0,1},{1,0},{2,3},{3,2},{4,5},{5,4},{6,7},{7,6},{8,9},{9,8},{10,11... | collective-permute-start | bytes 1572872 | tf_op jit(solution)/shard_map/ppermute | solution.py:842
  23.6 18.0 %collective-permute-start = (s32[4]{0:T(128)S(1)}, s32[4]{0:T(128)S(1)}, u32[]{:S(2)}, u32[]{:S(2)}) collective-permute-start(s32[4]{0:T(128)S(1)} %compare_select_fusion.1), channel_id=1, source_target_pairs={{0,4},{4,0},{8,12},{12,8},{16,20},{20,16},{24,28},{28,24},{1,5},{5... | collective-permute-start | bytes 56 | tf_op jit(solution)/shard_map/ppermute | solution.py:842
  26.2 13.8 %copy-start.91 = (bf16[1024,1024]{1,0:T(8,128)(2,1)S(1)}, bf16[1024,1024]{1,0:T(8,128)(2,1)}, u32[]{:S(2)}) copy-start(bf16[1024,1024]{1,0:T(8,128)(2,1)} %param.27) | copy-start | bytes 6291460
  26.3 15.4 %collective-permute-start.4 = (bf16[256,1024]{1,0:T(8,128)(2,1)S(1)}, bf16[256,1024]{1,0:T(8,128)(2,1)S(1)}, u32[]{:S(2)}, u32[]{:S(2)}) collective-permute-start(bf16[256,1024]{1,0:T(8,128)(2,1)S(1)} %add_convert_fusion.9.sum_ref), channel_id=1, source_target_pairs={{0,2},{1,3},{2,0},{3,1},{4,6},{5,7},{6,4},{7,5},{8,10},{9,11},{10,... | collective-permute-start | bytes 1572872 | tf_op jit(solution)/shard_map/ppermute | solution.py:842
  40.0 2.0 collective-permute-start.5
  42.2 22.4 %collective-permute-start.6 = (bf16[256,1024]{1,0:T(8,128)(2,1)S(1)}, bf16[256,1024]{1,0:T(8,128)(2,1)S(1)}, u32[]{:S(2)}, u32[]{:S(2)}) collective-permute-start(bf16[256,1024]{1,0:T(8,128)(2,1)S(1)} %add_convert_fusion.8.sum_ref), channel_id=1, source_target_pairs={{0,2},{1,3},{2,0},{3,1},{4,6},{5,7},{6,4},{7,5},{8,10},{9,11},{10,... | collective-permute-start | bytes 1572872 | tf_op jit(solution)/shard_map/ppermute | solution.py:842
  42.8 16.4 %copy-start.13 = (f32[3,1024]{1,0:T(4,128)S(1)}, f32[3,1024]{1,0:T(4,128)}, u32[]{:S(2)}) copy-start(f32[3,1024]{1,0:T(4,128)} %gain_ref.19) | copy-start | bytes 36868
  42.8 16.4 %copy-start.20 = (f32[3,1024]{1,0:T(4,128)S(1)}, f32[3,1024]{1,0:T(4,128)}, u32[]{:S(2)}) copy-start(f32[3,1024]{1,0:T(4,128)} %shift_ref.11) | copy-start | bytes 36868
  59.7 5.4 %collective-permute-start.7 = (bf16[256,1024]{1,0:T(8,128)(2,1)S(1)}, bf16[256,1024]{1,0:T(8,128)(2,1)S(1)}, u32[]{:S(2)}, u32[]{:S(2)}) collective-permute-start(bf16[256,1024]{1,0:T(8,128)(2,1)S(1)} %get-tuple-element.170.hm_ref), channel_id=1, source_target_pairs={{0,1},{1,0},{2,3},{3,2},{4,5},{5,4},{6,7},{7,6},{8,9},{9,8},{10,11... | collective-permute-start | bytes 1572872 | tf_op jit(solution)/shard_map/ppermute | solution.py:842
  70.8 2.3 collective-permute-start.9
  71.3 3.7 %collective-permute-start.8 = (bf16[256,1024]{1,0:T(8,128)(2,1)S(1)}, bf16[256,1024]{1,0:T(8,128)(2,1)S(1)}, u32[]{:S(2)}, u32[]{:S(2)}) collective-permute-start(bf16[256,1024]{1,0:T(8,128)(2,1)S(1)} %get-tuple-element.174.hm_ref), channel_id=1, source_target_pairs={{0,1},{1,0},{2,3},{3,2},{4,5},{5,4},{6,7},{7,6},{8,9},{9,8},{10,11... | collective-permute-start | bytes 1572872 | tf_op jit(solution)/shard_map/ppermute | solution.py:842
  71.4 3.6 %collective-permute-start.1 = (s32[4]{0:T(128)S(1)}, s32[4]{0:T(128)S(1)}, u32[]{:S(2)}, u32[]{:S(2)}) collective-permute-start(s32[4]{0:T(128)S(1)} %fusion.1), channel_id=1, source_target_pairs={{0,8},{4,12},{8,0},{12,4},{16,24},{20,28},{24,16},{28,20},{1,9},{5... | collective-permute-start | bytes 56 | tf_op jit(solution)/shard_map/ppermute | solution.py:842
  73.2 14.1 %collective-permute-start.12 = (bf16[256,1024]{1,0:T(8,128)(2,1)S(1)}, bf16[256,1024]{1,0:T(8,128)(2,1)S(1)}, u32[]{:S(2)}, u32[]{:S(2)}) collective-permute-start(bf16[256,1024]{1,0:T(8,128)(2,1)S(1)} %add_convert_fusion.7.sum_ref), channel_id=1, source_target_pairs={{0,2},{1,3},{2,0},{3,1},{4,6},{5,7},{6,4},{7,5},{8,10},{9,11},{10,... | collective-permute-start | bytes 1572872 | tf_op jit(solution)/shard_map/ppermute | solution.py:842
  84.1 4.7 %collective-permute-start.10 = (bf16[256,1024]{1,0:T(8,128)(2,1)S(1)}, bf16[256,1024]{1,0:T(8,128)(2,1)S(1)}, u32[]{:S(2)}, u32[]{:S(2)}) collective-permute-start(bf16[256,1024]{1,0:T(8,128)(2,1)S(1)} %get-tuple-element.180), channel_id=1, source_target_pairs={{0,1},{1,0},{2,3},{3,2},{4,5},{5,4},{6,7},{7,6},{8,9},{9,8},{10,11... | collective-permute-start | bytes 1572872 | tf_op jit(solution)/shard_map/ppermute | solution.py:842
  88.8 1.9 collective-permute-start.13
  89.0 14.4 %collective-permute-start.11 = (bf16[256,1024]{1,0:T(8,128)(2,1)S(1)}, bf16[256,1024]{1,0:T(8,128)(2,1)S(1)}, u32[]{:S(2)}, u32[]{:S(2)}) collective-permute-start(bf16[256,1024]{1,0:T(8,128)(2,1)S(1)} %add_convert_fusion.6.sum_ref), channel_id=1, source_target_pairs={{0,2},{1,3},{2,0},{3,1},{4,6},{5,7},{6,4},{7,5},{8,10},{9,11},{10,... | collective-permute-start | bytes 1572872 | tf_op jit(solution)/shard_map/ppermute | solution.py:842
  96.4 11.3 %copy-start.9 = (f32[2,256,1024]{2,1,0:T(8,128)}, f32[2,256,1024]{2,1,0:T(8,128)S(1)}, u32[]{:S(2)}) copy-start(f32[2,256,1024]{2,1,0:T(8,128)S(1)} %get-tuple-element.228.slope_ref) | copy-start | bytes 6291460
  96.4 11.3 %copy-start.16 = (bf16[2,256,1024]{2,1,0:T(8,128)(2,1)}, bf16[2,256,1024]{2,1,0:T(8,128)(2,1)S(1)}, u32[]{:S(2)}) copy-start(bf16[2,256,1024]{2,1,0:T(8,128)(2,1)S(1)} %get-tuple-element.227.g_ref) | copy-start | bytes 3145732
  96.5 10.3 %collective-permute-start.14 = (bf16[256,1024]{1,0:T(8,128)(2,1)S(1)}, bf16[256,1024]{1,0:T(8,128)(2,1)S(1)}, u32[]{:S(2)}, u32[]{:S(2)}) collective-permute-start(bf16[256,1024]{1,0:T(8,128)(2,1)S(1)} %get-tuple-element.190), channel_id=1, source_target_pairs={{0,1},{1,0},{2,3},{3,2},{4,5},{5,4},{6,7},{7,6},{8,9},{9,8},{10,11... | collective-permute-start | bytes 1572872 | tf_op jit(solution)/shard_map/ppermute | solution.py:842
  103.9 12.1 %copy-start.21 = (bf16[256,1024]{1,0:T(8,128)(2,1)}, bf16[256,1024]{1,0:T(8,128)(2,1)S(1)}, u32[]{:S(2)}) copy-start(bf16[256,1024]{1,0:T(8,128)(2,1)S(1)} %get-tuple-element.192.hm_ref) | copy-start | bytes 1572868
  103.9 5.8 %collective-permute-start.15 = (bf16[256,1024]{1,0:T(8,128)(2,1)S(1)}, bf16[256,1024]{1,0:T(8,128)(2,1)S(1)}, u32[]{:S(2)}, u32[]{:S(2)}) collective-permute-start(bf16[256,1024]{1,0:T(8,128)(2,1)S(1)} %get-tuple-element.192.hm_ref), channel_id=1, source_target_pairs={{0,1},{1,0},{2,3},{3,2},{4,5},{5,4},{6,7},{7,6},{8,9},{9,8},{10,11... | collective-permute-start | bytes 1572872 | tf_op jit(solution)/shard_map/ppermute | solution.py:842
  103.9 5.1 %collective-permute-start.2 = (s32[4]{0:T(128)S(1)}, s32[4]{0:T(128)S(1)}, u32[]{:S(2)}, u32[]{:S(2)}) collective-permute-start(s32[4]{0:T(128)S(1)} %fusion.5), channel_id=1, source_target_pairs={{0,16},{4,20},{8,24},{12,28},{16,0},{20,4},{24,8},{28,12},{1,17},{... | collective-permute-start | bytes 56 | tf_op jit(solution)/shard_map/ppermute | solution.py:842
  107.8 14.4 %collective-permute-start.17 = (bf16[256,1024]{1,0:T(8,128)(2,1)}, bf16[256,1024]{1,0:T(8,128)(2,1)}, u32[]{:S(2)}, u32[]{:S(2)}) collective-permute-start(bf16[256,1024]{1,0:T(8,128)(2,1)} %add_convert_fusion.5.sum_ref), channel_id=1, source_target_pairs={{0,2},{1,3},{2,0},{3,1},{4,6},{5,7},{6,4},{7,5},{8,10},{9,11},{10,... | collective-permute-start | bytes 1572872 | tf_op jit(solution)/shard_map/ppermute | solution.py:842
  120.6 5.2 %collective-permute-start.16 = (bf16[256,1024]{1,0:T(8,128)(2,1)}, bf16[256,1024]{1,0:T(8,128)(2,1)}, u32[]{:S(2)}, u32[]{:S(2)}) collective-permute-start(bf16[256,1024]{1,0:T(8,128)(2,1)} %get-tuple-element.194), channel_id=1, source_target_pairs={{0,1},{1,0},{2,3},{3,2},{4,5},{5,4},{6,7},{7,6},{8,9},{9,8},{10,11... | collective-permute-start | bytes 1572872 | tf_op jit(solution)/shard_map/ppermute | solution.py:842
  125.2 3.2 %collective-permute-start.18 = (bf16[256,1024]{1,0:T(8,128)(2,1)}, bf16[256,1024]{1,0:T(8,128)(2,1)S(1)}, u32[]{:S(2)}, u32[]{:S(2)}) collective-permute-start(bf16[256,1024]{1,0:T(8,128)(2,1)} %copy-done.72), channel_id=1, source_target_pairs={{0,1},{1,0},{2,3},{3,2},{4,5},{5,4},{6,7},{7,6},{8,9},{9,8},{10,11... | collective-permute-start | bytes 1572872 | tf_op jit(solution)/shard_map/ppermute | solution.py:842
  125.3 5.7 %collective-permute-start.20 = (bf16[256,1024]{1,0:T(8,128)(2,1)S(1)}, bf16[256,1024]{1,0:T(8,128)(2,1)S(1)}, u32[]{:S(2)}, u32[]{:S(2)}) collective-permute-start(bf16[256,1024]{1,0:T(8,128)(2,1)S(1)} %get-tuple-element.206.hm_ref.h_ref), channel_id=1, source_target_pairs={{0,1},{1,0},{2,3},{3,2},{4,5},{5,4},{6,7},{7,6},{8,9},{9,8},{10,11... | collective-permute-start | bytes 1572872 | tf_op jit(solution)/shard_map/ppermute | solution.py:842
  125.8 3.7 %collective-permute-start.19 = (bf16[256,1024]{1,0:T(8,128)(2,1)S(1)}, bf16[256,1024]{1,0:T(8,128)(2,1)S(1)}, u32[]{:S(2)}, u32[]{:S(2)}) collective-permute-start(bf16[256,1024]{1,0:T(8,128)(2,1)S(1)} %copy-done.71), channel_id=1, source_target_pairs={{0,1},{1,0},{2,3},{3,2},{4,5},{5,4},{6,7},{7,6},{8,9},{9,8},{10,11... | collective-permute-start | bytes 1572872 | tf_op jit(solution)/shard_map/ppermute | solution.py:842
  127.1 48.0 %collective-permute-start.23 = (bf16[256,1024]{1,0:T(8,128)(2,1)S(1)}, bf16[256,1024]{1,0:T(8,128)(2,1)S(1)}, u32[]{:S(2)}, u32[]{:S(2)}) collective-permute-start(bf16[256,1024]{1,0:T(8,128)(2,1)S(1)} %add_convert_fusion.4.sum_ref), channel_id=1, source_target_pairs={{0,2},{1,3},{2,0},{3,1},{4,6},{5,7},{6,4},{7,5},{8,10},{9,11},{10,... | collective-permute-start | bytes 1572872 | tf_op jit(solution)/shard_map/ppermute | solution.py:842
  128.6 46.4 %collective-permute-start.21 = (bf16[256,1024]{1,0:T(8,128)(2,1)S(1)}, bf16[256,1024]{1,0:T(8,128)(2,1)S(1)}, u32[]{:S(2)}, u32[]{:S(2)}) collective-permute-start(bf16[256,1024]{1,0:T(8,128)(2,1)S(1)} %add_convert_fusion.3.row_ref), channel_id=1, source_target_pairs={{0,2},{1,3},{2,0},{3,1},{4,6},{5,7},{6,4},{7,5},{8,10},{9,11},{10,... | collective-permute-start | bytes 1572872 | tf_op jit(solution)/shard_map/ppermute | solution.py:842
  129.6 45.4 %collective-permute-start.22 = (bf16[256,1024]{1,0:T(8,128)(2,1)S(1)}, bf16[256,1024]{1,0:T(8,128)(2,1)S(1)}, u32[]{:S(2)}, u32[]{:S(2)}) collective-permute-start(bf16[256,1024]{1,0:T(8,128)(2,1)S(1)} %add_convert_fusion.2.row_ref), channel_id=1, source_target_pairs={{0,2},{1,3},{2,0},{3,1},{4,6},{5,7},{6,4},{7,5},{8,10},{9,11},{10,... | collective-permute-start | bytes 1572872 | tf_op jit(solution)/shard_map/ppermute | solution.py:842
  175.0 2.0 collective-permute-start.24
  175.6 2.8 collective-permute-start.25
  177.5 35.4 %collective-permute-start.28 = (bf16[272,1024]{1,0:T(8,128)(2,1)S(1)}, bf16[272,1024]{1,0:T(8,128)(2,1)S(1)}, u32[]{:S(2)}, u32[]{:S(2)}) collective-permute-start(bf16[272,1024]{1,0:T(8,128)(2,1)S(1)} %get-tuple-element.214.total_ref), channel_id=1, source_target_pairs={{0,2},{1,3},{2,0},{3,1},{4,6},{5,7},{6,4},{7,5},{8,10},{9,11},{10,... | collective-permute-start | bytes 1671176 | tf_op jit(solution)/shard_map/ppermute | solution.py:842
  178.4 38.4 %copy-start.30 = (bf16[256,1024]{1,0:T(8,128)(2,1)S(1)}, bf16[256,1024]{1,0:T(8,128)(2,1)}, u32[]{:S(2)}) copy-start(bf16[256,1024]{1,0:T(8,128)(2,1)} %copy-done.29) | copy-start | bytes 1572868
  178.4 38.4 %copy-start.32 = (bf16[256,1024]{1,0:T(8,128)(2,1)S(1)}, bf16[256,1024]{1,0:T(8,128)(2,1)}, u32[]{:S(2)}) copy-start(bf16[256,1024]{1,0:T(8,128)(2,1)} %copy-done.31) | copy-start | bytes 1572868
  178.4 38.4 %copy-start.50 = (bf16[2,256,16]{2,1,0:T(8,128)(2,1)S(1)}, bf16[2,256,16]{2,1,0:T(8,128)(2,1)}, u32[]{:S(2)}) copy-start(bf16[2,256,16]{2,1,0:T(8,128)(2,1)} %copy-done.49) | copy-start | bytes 49156
  212.9 2.1 collective-permute-start.26
  214.4 2.3 collective-permute-start.29
  215.5 14.7 %collective-permute-start.27 = (bf16[272,1024]{1,0:T(8,128)(2,1)S(1)}, bf16[272,1024]{1,0:T(8,128)(2,1)S(1)}, u32[]{:S(2)}, u32[]{:S(2)}) collective-permute-start(bf16[272,1024]{1,0:T(8,128)(2,1)S(1)} %get-tuple-element.219.total_ref), channel_id=1, source_target_pairs={{0,2},{1,3},{2,0},{3,1},{4,6},{5,7},{6,4},{7,5},{8,10},{9,11},{10,... | collective-permute-start | bytes 1671176 | tf_op jit(solution)/shard_map/ppermute | solution.py:842
  223.0 8.6 %collective-permute-start.30 = (bf16[256,1024]{1,0:T(8,128)(2,1)S(1)}, bf16[256,1024]{1,0:T(8,128)(2,1)S(1)}, u32[]{:S(2)}, u32[]{:S(2)}) collective-permute-start(bf16[256,1024]{1,0:T(8,128)(2,1)S(1)} %get-tuple-element.233), channel_id=1, source_target_pairs={{0,1},{1,0},{2,3},{3,2},{4,5},{5,4},{6,7},{7,6},{8,9},{9,8},{10,11... | collective-permute-start | bytes 1572872 | tf_op jit(solution)/shard_map/ppermute | solution.py:842
  231.5 2.0 collective-permute-start.31
  231.8 14.4 %collective-permute-start.32 = (bf16[256,1024]{1,0:T(8,128)(2,1)S(1)}, bf16[256,1024]{1,0:T(8,128)(2,1)S(1)}, u32[]{:S(2)}, u32[]{:S(2)}) collective-permute-start(bf16[256,1024]{1,0:T(8,128)(2,1)S(1)} %add_convert_fusion.1.sum_ref), channel_id=1, source_target_pairs={{0,2},{1,3},{2,0},{3,1},{4,6},{5,7},{6,4},{7,5},{8,10},{9,11},{10,... | collective-permute-start | bytes 1572872 | tf_op jit(solution)/shard_map/ppermute | solution.py:842
  233.5 12.6 %copy-start.6 = (f32[256,1024]{1,0:T(8,128)S(1)}, f32[256,1024]{1,0:T(8,128)}, u32[]{:S(2)}) copy-start(f32[256,1024]{1,0:T(8,128)} %copy-done.4) | copy-start | bytes 3145732
  239.9 8.1 %collective-permute-start.33 = (bf16[256,1024]{1,0:T(8,128)(2,1)S(1)}, bf16[256,1024]{1,0:T(8,128)(2,1)S(1)}, u32[]{:S(2)}, u32[]{:S(2)}) collective-permute-start(bf16[256,1024]{1,0:T(8,128)(2,1)S(1)} %get-tuple-element.244), channel_id=1, source_target_pairs={{0,1},{1,0},{2,3},{3,2},{4,5},{5,4},{6,7},{7,6},{8,9},{9,8},{10,11... | collective-permute-start | bytes 1572872 | tf_op jit(solution)/shard_map/ppermute | solution.py:842
  247.9 2.0 collective-permute-start.34
  248.2 14.4 %collective-permute-start.35 = (bf16[256,1024]{1,0:T(8,128)(2,1)S(1)}, bf16[256,1024]{1,0:T(8,128)(2,1)S(1)}, u32[]{:S(2)}, u32[]{:S(2)}) collective-permute-start(bf16[256,1024]{1,0:T(8,128)(2,1)S(1)} %add_convert_fusion.sum_ref), channel_id=1, source_target_pairs={{0,2},{1,3},{2,0},{3,1},{4,6},{5,7},{6,4},{7,5},{8,10},{9,11},{10,... | collective-permute-start | bytes 1572872 | tf_op jit(solution)/shard_map/ppermute | solution.py:842
  264.3 1.9 collective-permute-start.36
  277.7 25.7 %copy-start.40 = (f32[4096,4]{0,1:T(4,128)S(1)}, f32[4096,4]{0,1:T(4,128)}, u32[]{:S(2)}) copy-start(f32[4096,4]{0,1:T(4,128)} %param.35) | copy-start | bytes 196612
  277.7 25.7 %copy-start.42 = (f32[4,4096]{1,0:T(4,128)S(1)}, f32[4,4096]{1,0:T(4,128)}, u32[]{:S(2)}) copy-start(f32[4,4096]{1,0:T(4,128)} %refs_3_.1) | copy-start | bytes 196612
  277.7 25.7 %copy-start.59 = (f32[5,1024,4]{1,2,0:T(4,128)S(1)}, f32[5,1024,4]{1,2,0:T(4,128)}, u32[]{:S(2)}) copy-start(f32[5,1024,4]{1,2,0:T(4,128)} %param.38) | copy-start | bytes 245764
  277.7 25.7 %copy-start.60 = (f32[5,4,1024]{2,1,0:T(4,128)S(1)}, f32[5,4,1024]{2,1,0:T(4,128)}, u32[]{:S(2)}) copy-start(f32[5,4,1024]{2,1,0:T(4,128)} %refs_6_.1) | copy-start | bytes 245764
  277.7 25.7 %copy-start.61 = (f32[5,1024,4]{1,2,0:T(4,128)S(1)}, f32[5,1024,4]{1,2,0:T(4,128)}, u32[]{:S(2)}) copy-start(f32[5,1024,4]{1,2,0:T(4,128)} %param.42) | copy-start | bytes 245764
  277.7 25.7 %copy-start.62 = (f32[5,4,1024]{2,1,0:T(4,128)S(1)}, f32[5,4,1024]{2,1,0:T(4,128)}, u32[]{:S(2)}) copy-start(f32[5,4,1024]{2,1,0:T(4,128)} %refs_10_.1) | copy-start | bytes 245764
  277.7 25.7 %copy-start.63 = (f32[4096,4]{0,1:T(4,128)S(1)}, f32[4096,4]{0,1:T(4,128)}, u32[]{:S(2)}) copy-start(f32[4096,4]{0,1:T(4,128)} %param.39) | copy-start | bytes 196612
  277.7 25.7 %copy-start.64 = (f32[4,4096]{1,0:T(4,128)S(1)}, f32[4,4096]{1,0:T(4,128)}, u32[]{:S(2)}) copy-start(f32[4,4096]{1,0:T(4,128)} %refs_7_.1) | copy-start | bytes 196612
  277.8 25.7 %copy-start.65 = (f32[4096,4]{0,1:T(4,128)S(1)}, f32[4096,4]{0,1:T(4,128)}, u32[]{:S(2)}) copy-start(f32[4096,4]{0,1:T(4,128)} %param.43) | copy-start | bytes 196612
  277.8 25.7 %copy-start.66 = (f32[4,4096]{1,0:T(4,128)S(1)}, f32[4,4096]{1,0:T(4,128)}, u32[]{:S(2)}) copy-start(f32[4,4096]{1,0:T(4,128)} %refs_11_.1) | copy-start | bytes 196612
  277.8 1.3 collective-permute-start.37
  279.2 3.9 %collective-permute-start.38 = (f32[4,1536]{1,0:T(4,128)S(1)}, f32[4,1536]{1,0:T(4,128)S(1)}, u32[]{:S(2)}, u32[]{:S(2)}) collective-permute-start(f32[4,1536]{1,0:T(4,128)S(1)} %constant_dynamic-slice_fusion), channel_id=1, source_target_pairs={{0,2},{1,3},{2,0},{3,1},{4,6},{5,7},{6,4},{7,5},{8,10},{9,11},{10,... | collective-permute-start | bytes 73736 | tf_op jit(solution)/shard_map/ppermute | solution.py:842
  283.1 4.4 %collective-permute-start.39 = (f32[4,4736]{1,0:T(4,128)S(1)}, f32[4,4736]{1,0:T(4,128)S(1)}, u32[]{:S(2)}, u32[]{:S(2)}) collective-permute-start(f32[4,4736]{1,0:T(4,128)S(1)} %pad_maximum_fusion), channel_id=1, source_target_pairs={{0,4},{4,0},{8,12},{12,8},{16,20},{20,16},{24,28},{28,24},{1,5},{5... | collective-permute-start | bytes 227336 | tf_op jit(solution)/shard_map/ppermute | solution.py:842
  287.6 4.4 %collective-permute-start.40 = (f32[4,4736]{1,0:T(4,128)S(1)}, f32[4,4736]{1,0:T(4,128)S(1)}, u32[]{:S(2)}, u32[]{:S(2)}) collective-permute-start(f32[4,4736]{1,0:T(4,128)S(1)} %fusion.2), channel_id=1, source_target_pairs={{0,8},{4,12},{8,0},{12,4},{16,24},{20,28},{24,16},{28,20},{1,9},{5... | collective-permute-start | bytes 227336 | tf_op jit(solution)/shard_map/ppermute | solution.py:842
  292.0 5.3 %collective-permute-start.41 = (f32[4,4736]{1,0:T(4,128)S(1)}, f32[4,4736]{1,0:T(4,128)S(1)}, u32[]{:S(2)}, u32[]{:S(2)}) collective-permute-start(f32[4,4736]{1,0:T(4,128)S(1)} %add.100), channel_id=1, source_target_pairs={{0,16},{4,20},{8,24},{12,28},{16,0},{20,4},{24,8},{28,12},{1,17},{... | collective-permute-start | bytes 227336 | tf_op jit(solution)/shard_map/ppermute | solution.py:842
  297.4 4.4 %collective-permute-start.42 = (f32[1,4,4736]{2,1,0:T(4,128)S(1)}, f32[1,4,4736]{2,1,0:T(4,128)S(1)}, u32[]{:S(2)}, u32[]{:S(2)}) collective-permute-start(f32[1,4,4736]{2,1,0:T(4,128)S(1)} %add_bitcast_fusion), channel_id=1, source_target_pairs={{0,2},{1,3},{2,0},{3,1},{4,6},{5,7},{6,4},{7,5},{8,10},{9,11},{10,... | collective-permute-start | bytes 227336 | tf_op jit(solution)/shard_map/ppermute | solution.py:842
  301.9 1.4 collective-permute-start.43
  (72 other events, 280.6 us)
